TPU v7x, 32 devices: a whole 2x2x4 slice. The times are simulated.
32 devices in a mesh: row: 4 (over y, x), col: 8 (over z, core).
Axes of the slice: x: 2, y: 2, z: 4, core: 2. Of those that a mesh axis runs over, the one named last changes fastest.
Arguments:
- transmission: float32 [2, 1024, 2048], P(None, 'row', 'col'), may hold values from -5 to 5
- probe_modes: float32 [2, 2, 256, 256], replicated, may hold values from -5 to 5
- measured: float32 [64, 256, 256], P(('row', 'col')), may hold values from 0.2 to 8
- offset_down: int32 [64], P(('row', 'col')), may hold values from 0 to 255, as said below
- offset_across: int32 [64], P(('row', 'col')), may hold values from 0 to 255, as said below
Outputs:
- object_gradient: float32 [2, 1024, 2048], P(None, 'row', 'col')
- probe_gradient: float32 [2, 2, 256, 256], replicated
Inputs may be any that keep to these rules, and one draw needn't show every extreme that they name: `offset_down`: offset of the scan's window start inside the tile of the device that holds the scan; a window reaches at most into the next tile down, the next tile across and the tile diagonally beyond. `offset_across`: as offset_down, along columns.
All inputs are finite; a program needn't handle non-finite values.
Results may differ from a plain program's by a relative error of at most 0.0001.
Values sent between devices are 32-bit elements; how exact they have to be, the bound alone decides.
No kernel may reach another device: no remote copies, remote signals or barrier semaphores. Data moves between devices by JAX's collectives and lax.ppermute only.
A program may use at most 64 MiB of HBM per device.

v0:
```python
import math

import jax
import jax.numpy as jnp
import numpy as np
from jax import lax
from jax.experimental import pallas as pl
from jax.experimental.pallas import tpu as pltpu
from jax.sharding import PartitionSpec as P


VMEM = pltpu.VMEM
SMEM = pltpu.SMEM
PREPARE_VMEM = 8 * 1024 * 1024
PROCESS_VMEM = 20 * 1024 * 1024


def shifted(block, axis, distance):
    count = lax.axis_size(axis)
    route = [(i - distance, i) for i in range(count) if 0 <= i - distance < count]
    return lax.ppermute(block, axis, route)


def swapped(block, axis, mask):
    return lax.ppermute(block, axis, [(i, i ^ mask) for i in range(lax.axis_size(axis))])


def power_of_two(number):
    return number & (number - 1) == 0


def chip_groups(parts):
    rows, cols = lax.axis_size("row"), lax.axis_size("col")
    return [
        [row * cols + first + core + 2 * part for row in range(rows) for part in range(parts)]
        for first in range(0, cols, 2 * parts)
        for core in range(2)
    ]


def scatter_sum(values, groups):
    count = len(groups[0])
    pieces = values.reshape((count, values.shape[0] // count) + values.shape[1:])
    return jnp.sum(
        lax.all_to_all(pieces, ("row", "col"), 0, 0, axis_index_groups=groups), axis=0
    )


def gather_slices(piece, groups):
    copies = jnp.broadcast_to(piece[None], (len(groups[0]),) + piece.shape)
    slices = lax.all_to_all(copies, ("row", "col"), 0, 0, axis_index_groups=groups)
    return slices.reshape((-1,) + piece.shape[1:])


def sum_over_groups(piece, stride):
    count = lax.axis_size("col")
    if power_of_two(count // stride):
        mask = stride
        while mask < count:
            piece = piece + swapped(piece, "col", mask)
            mask *= 2
        return piece
    groups = [list(range(first, count, stride)) for first in range(stride)]
    copies = jnp.broadcast_to(piece[None], (count // stride,) + piece.shape)
    return jnp.sum(lax.all_to_all(copies, "col", 0, 0, axis_index_groups=groups), axis=0)


def split_table(table):
    high = table.astype(jnp.bfloat16)
    low = (table - high.astype(np.float64)).astype(jnp.bfloat16)
    return high, low


def tables(length):
    half = length // 2
    counter = np.arange(half)
    angles = 2.0 * math.pi * (np.outer(counter, counter) % half) / half
    cosines = np.cos(angles) / math.sqrt(length)
    sines = np.sin(angles) / math.sqrt(length)
    forward = np.block([[cosines, -sines], [sines, cosines]])
    backward = np.block([[cosines, sines], [-sines, cosines]])
    result = {}
    for name, table in (("f", forward), ("b", backward)):
        high, low = split_table(table)
        result["right_" + name] = np.concatenate([high, high, low], axis=0)
        high, low = split_table(np.ascontiguousarray(table.T))
        result["left_" + name] = np.concatenate([high, high, low], axis=1)
    turn = 2.0 * math.pi * counter / length
    result["lane"] = np.stack([np.cos(turn), np.sin(turn)]).astype(np.float32)
    across = np.stack([np.cos(turn), np.sin(turn)]).astype(np.float32)
    result["sub"] = np.ascontiguousarray(np.repeat(across[:, :, None], half, axis=2))
    order = np.concatenate([np.arange(0, length, 2), np.arange(1, length, 2)])
    select = np.zeros((length, length), np.float32)
    select[order, np.arange(length)] = 1.0
    result["pick_cols"] = np.concatenate([select] * 3, axis=0).astype(jnp.bfloat16)
    result["pick_rows"] = np.concatenate([select.T] * 3, axis=1).astype(jnp.bfloat16)
    return result


def halves(values):
    high = values.astype(jnp.bfloat16)
    low = (values - high.astype(jnp.float32)).astype(jnp.bfloat16)
    return high, low


def dot(left, right):
    return jnp.dot(left, right, preferred_element_type=jnp.float32)


def thirds(values):
    high = values.astype(jnp.bfloat16)
    rest = values - high.astype(jnp.float32)
    middle = rest.astype(jnp.bfloat16)
    low = (rest - middle.astype(jnp.float32)).astype(jnp.bfloat16)
    return [high, middle, low]


def prepare_kernel(measured_ref, pick_rows_ref, pick_cols_ref, *refs):
    out_ref = refs[-1]
    for source, target in zip(refs[: len(refs) // 2], refs[len(refs) // 2 :]):
        target[...] = source[...]
    scans, length, _ = measured_ref.shape
    half = length // 2
    for which in range(scans):
        rows = dot(pick_rows_ref[...], jnp.concatenate(thirds(measured_ref[which]), axis=0))
        both = dot(jnp.concatenate(thirds(rows), axis=1), pick_cols_ref[...])
        out_ref[which, :, :length] = both[:half]
        out_ref[which, :, length:] = both[half:]


def scan_kernel(
    down_ref,
    across_ref,
    own_ref,
    right_ref,
    below_ref,
    corner_ref,
    relayed_ref,
    probe_ref,
    measured_ref,
    right_f_ref,
    left_f_ref,
    left_b_ref,
    right_b_ref,
    lane_ref,
    sub_ref,
    own_out,
    right_out,
    below_out,
    corner_out,
    keep_out,
    send_out,
    wave_ref,
):
    scans = measured_ref.shape[0]
    modes, _, length, _ = probe_ref.shape
    half = length // 2
    core = lax.rem(lax.axis_index("col"), 2)
    row_of = lax.broadcasted_iota(jnp.int32, (length, length), 0)
    col_of = lax.broadcasted_iota(jnp.int32, (length, length), 1)

    def apply_right(parts, table_ref):
        high, low = halves(parts)
        return dot(jnp.concatenate([high, low, high], axis=1), table_ref[...])

    def apply_left(table_ref, parts):
        high, low = halves(parts)
        return dot(table_ref[...], jnp.concatenate([high, low, high], axis=0))

    def lane_turn():
        return lane_ref[0:1, :], lane_ref[1:2, :]

    for which in range(scans):
        down = down_ref[which]
        across = across_ref[which]
        later_row = row_of < down
        later_col = col_of < across
        up = lax.rem(length - down, length)
        back_across = lax.rem(length - across, length)
        patch = []
        for part in range(2):
            merged = jnp.where(
                later_row,
                jnp.where(later_col, corner_ref[part] + relayed_ref[part], below_ref[part]),
                jnp.where(later_col, right_ref[part], own_ref[part]),
            )
            patch.append(pltpu.roll(pltpu.roll(merged, up, 0), back_across, 1))
        patch_r, patch_i = patch

        intensity = None
        for step in range(modes):
            mode = step ^ core
            probe_r, probe_i = probe_ref[mode, 0], probe_ref[mode, 1]
            exit_r = probe_r * patch_r - probe_i * patch_i
            exit_i = probe_r * patch_i + probe_i * patch_r
            cos, sin = lane_turn()
            first_r, last_r = exit_r[:, :half], exit_r[:, half:]
            first_i, last_i = exit_i[:, :half], exit_i[:, half:]
            gap_r, gap_i = first_r - last_r, first_i - last_i
            even = jnp.concatenate([first_r + last_r, first_i + last_i], axis=1)
            odd = jnp.concatenate(
                [gap_r * cos + gap_i * sin, gap_i * cos - gap_r * sin], axis=1
            )
            even = apply_right(even, right_f_ref)
            odd = apply_right(odd, right_f_ref)
            cos, sin = sub_ref[0], sub_ref[1]
            sums, turned = [[], []], [[], []]
            for block in (even, odd):
                top_r, low_r = block[:half, :half], block[half:, :half]
                top_i, low_i = block[:half, half:], block[half:, half:]
                gap_r, gap_i = top_r - low_r, top_i - low_i
                sums[0].append(top_r + low_r)
                sums[1].append(top_i + low_i)
                turned[0].append(gap_r * cos + gap_i * sin)
                turned[1].append(gap_i * cos - gap_r * sin)
            stacked = jnp.concatenate(
                [jnp.concatenate(sums[part] + turned[part], axis=1) for part in range(2)], axis=0
            )
            wave = apply_left(left_f_ref, stacked)
            wave_ref[step] = wave
            wave_r, wave_i = wave[:half], wave[half:]
            square = wave_r * wave_r + wave_i * wave_i
            intensity = square if intensity is None else intensity + square
        resid = intensity - measured_ref[which]

        object_r = object_i = None
        for step in range(modes):
            mode = step ^ core
            wave = wave_ref[step]
            weighted = jnp.concatenate([resid * wave[:half], resid * wave[half:]], axis=0)
            rows = apply_left(left_b_ref, weighted)
            cos, sin = sub_ref[0], sub_ref[1]
            cos = jnp.concatenate([cos, cos], axis=1)
            sin = jnp.concatenate([sin, sin], axis=1)
            even_r, odd_r = rows[:half, :length], rows[:half, length:]
            even_i, odd_i = rows[half:, :length], rows[half:, length:]
            turn_r = odd_r * cos - odd_i * sin
            turn_i = odd_i * cos + odd_r * sin
            real = jnp.concatenate([even_r + turn_r, even_r - turn_r], axis=0)
            imag = jnp.concatenate([even_i + turn_i, even_i - turn_i], axis=0)
            even = jnp.concatenate([real[:, :half], imag[:, :half]], axis=1)
            odd = jnp.concatenate([real[:, half:], imag[:, half:]], axis=1)
            even = apply_right(even, right_b_ref)
            odd = apply_right(odd, right_b_ref)
            cos, sin = lane_turn()
            turn_r = odd[:, :half] * cos - odd[:, half:] * sin
            turn_i = odd[:, half:] * cos + odd[:, :half] * sin
            back_r = jnp.concatenate([even[:, :half] + turn_r, even[:, :half] - turn_r], axis=1)
            back_i = jnp.concatenate([even[:, half:] + turn_i, even[:, half:] - turn_i], axis=1)
            probe_out = (keep_out, send_out)[step]
            term_r = patch_r * back_r + patch_i * back_i
            term_i = patch_r * back_i - patch_i * back_r
            if which == 0:
                probe_out[0] = term_r
                probe_out[1] = term_i
            else:
                probe_out[0] = probe_out[0] + term_r
                probe_out[1] = probe_out[1] + term_i
            probe_r, probe_i = probe_ref[mode, 0], probe_ref[mode, 1]
            term_r = probe_r * back_r + probe_i * back_i
            term_i = probe_r * back_i - probe_i * back_r
            object_r = term_r if object_r is None else object_r + term_r
            object_i = term_i if object_i is None else object_i + term_i

        for part, values in ((0, object_r), (1, object_i)):
            placed = pltpu.roll(pltpu.roll(values, down, 0), across, 1)
            upper = jnp.where(later_row, 0.0, placed)
            lower = jnp.where(later_row, placed, 0.0)
            pieces = (
                (own_out, jnp.where(later_col, 0.0, upper)),
                (right_out, jnp.where(later_col, upper, 0.0)),
                (below_out, jnp.where(later_col, 0.0, lower)),
                (corner_out, jnp.where(later_col, lower, 0.0)),
            )
            for out, piece in pieces:
                if which == 0:
                    out[part] = piece
                else:
                    out[part] = out[part] + piece


def in_vmem(*arrays):
    return [pltpu.with_memory_space_constraint(array, VMEM) for array in arrays]


def whole():
    return pl.BlockSpec(memory_space=VMEM)


def prepare(measured, picks, consts):
    scans, length, _ = measured.shape
    shapes = [VMEM(const.shape, const.dtype) for const in consts]
    return pl.pallas_call(
        prepare_kernel,
        out_shape=shapes + [VMEM((scans, length // 2, 2 * length), jnp.float32)],
        in_specs=[whole()] * (3 + len(consts)),
        out_specs=[whole()] * (1 + len(consts)),
        compiler_params=pltpu.CompilerParams(vmem_limit_bytes=PREPARE_VMEM),
        name="prepare",
    )(measured, *picks, *consts)


def process_scans(offsets, tiles, probe_modes, measured, consts):
    modes, _, length, _ = probe_modes.shape
    operands = in_vmem(*tiles, probe_modes, measured, *consts)
    results = [tiles[0].shape] * 4 + [probe_modes.shape[1:]] * 2
    return pl.pallas_call(
        scan_kernel,
        out_shape=[VMEM(shape, jnp.float32) for shape in results],
        in_specs=[pl.BlockSpec(memory_space=SMEM)] * 2 + [whole()] * len(operands),
        out_specs=[whole()] * len(results),
        scratch_shapes=[VMEM((modes, length, 2 * length), jnp.float32)],
        compiler_params=pltpu.CompilerParams(vmem_limit_bytes=PROCESS_VMEM),
        name="process_scans",
    )(*offsets, *operands)


def on_device(transmission, probe_modes, measured, offset_down, offset_across):
    length = probe_modes.shape[-1]
    scan_count = measured.shape[0]
    rows, cols = lax.axis_size("row"), lax.axis_size("col")
    core = lax.rem(lax.axis_index("col"), 2)
    table = tables(length)

    below = shifted(transmission, "row", -1)
    direct = [
        ((row + 1) * cols + col + 1, row * cols + col)
        for row in range(rows - 1)
        for col in range(1, cols - 1, 2)
    ]
    corner = lax.ppermute(transmission, ("row", "col"), direct)
    right = shifted(transmission, "col", -1)
    consts = [table[name] for name in ("right_f", "left_f", "left_b", "right_b", "lane", "sub")]
    picks = [table["pick_rows"], table["pick_cols"]]
    *consts, ordered = prepare(measured, picks, consts)
    relayed = lax.ppermute(below, "col", [(col + 1, col) for col in range(0, cols - 1, 2)])

    offsets = (offset_down, offset_across)
    own, to_right, to_below, to_corner, keep, send = process_scans(
        offsets, (transmission, right, below, corner, relayed), probe_modes, ordered, consts
    )

    keep = keep + swapped(send, "col", 1)
    parts = 2 if cols % 4 == 0 else 1
    groups = chip_groups(parts)
    piece = scatter_sum(keep.reshape((-1, length)), groups)
    piece = sum_over_groups(piece, 2 * parts)
    scans_total = scan_count * rows * cols
    mine = gather_slices(piece * (1.0 / math.sqrt(scans_total)), groups).reshape(keep.shape)
    other = swapped(mine, "col", 1)
    probe_gradient = jnp.zeros(probe_modes.shape, jnp.float32)
    probe_gradient = lax.dynamic_update_index_in_dim(probe_gradient, mine, core, 0)
    probe_gradient = lax.dynamic_update_index_in_dim(probe_gradient, other, 1 - core, 0)

    to_below = to_below + shifted(to_corner, "col", 1)
    own = lax.optimization_barrier(own + shifted(to_right, "col", 1))
    own = own + shifted(to_below, "row", 1)
    return own, probe_gradient


def solution(mesh):
    in_specs = (
        P(None, "row", "col"),
        P(),
        P(("row", "col"), None, None),
        P(("row", "col")),
        P(("row", "col")),
    )
    out_specs = (P(None, "row", "col"), P())
    return jax.shard_map(
        on_device, mesh=mesh, in_specs=in_specs, out_specs=out_specs, check_vma=False
    )
```

profile of v0, /device:TPU:20, one launch (start us, length us, event | category | flops | bytes accessed | tf_op | source)
XLA Modules:
  0.0 97.5 jit_solution(12381484678874092681)
XLA Ops:
  0.6 0.0 copy-start.10
  0.6 0.0 copy-start
  0.7 3.5 %collective-permute-start.1 = (f32[2,256,256]{2,1,0:T(8,128)}, f32[2,256,256]{2,1,0:T(8,128)S(1)}, u32[]{:S(2)}, u32[]{:S(2)}) collective-permute-start(f32[2,256,256]{2,1,0:T(8,128)} %own_ref.1), channel_id=1, source_target_pairs={{8,0},{16,8},{24,16},{9,1},{17,9},{25,17},{10,2},{18,10},{26,18},{... | collective-permute-start | bytes 1572872 | tf_op jit(solution)/shard_map/ppermute | solution.py:21
  4.1 1.9 %collective-permute-start = (f32[2,256,256]{2,1,0:T(8,128)}, f32[2,256,256]{2,1,0:T(8,128)S(1)}, u32[]{:S(2)}, u32[]{:S(2)}) collective-permute-start(f32[2,256,256]{2,1,0:T(8,128)} %own_ref.1), channel_id=1, source_target_pairs={{1,0},{2,1},{3,2},{4,3},{5,4},{6,5},{7,6},{9,8},{10,9},{11,10},{12... | collective-permute-start | bytes 1572872 | tf_op jit(solution)/shard_map/ppermute | solution.py:21
  6.1 2.5 %collective-permute-start.2 = (f32[2,256,256]{2,1,0:T(8,128)}, f32[2,256,256]{2,1,0:T(8,128)S(1)}, u32[]{:S(2)}, u32[]{:S(2)}) collective-permute-start(f32[2,256,256]{2,1,0:T(8,128)} %own_ref.1), channel_id=1, source_target_pairs={{10,1},{12,3},{14,5},{18,9},{20,11},{22,13},{26,17},{28,19},{30,21}} | collective-permute-start | bytes 1572872 | tf_op jit(solution)/shard_map/ppermute | solution.py:331
  8.5 13.6 %collective-permute-done.1.below_ref = f32[2,256,256]{2,1,0:T(8,128)S(1)} collective-permute-done((f32[2,256,256]{2,1,0:T(8,128)}, f32[2,256,256]{2,1,0:T(8,128)S(1)}, u32[]{:S(2)}, u32[]{:S(2)}) %collective-permute-start.1) | collective-permute-done | bytes 524320 | tf_op jit(solution)/shard_map/ppermute | solution.py:21
  22.2 1.3 %collective-permute-start.3 = (f32[2,256,256]{2,1,0:T(8,128)S(1)}, f32[2,256,256]{2,1,0:T(8,128)S(1)}, u32[]{:S(2)}, u32[]{:S(2)}) collective-permute-start(f32[2,256,256]{2,1,0:T(8,128)S(1)} %collective-permute-done.1.below_ref), channel_id=1, source_target_pairs={{1,0},{3,2},{5,4},{7,6},{9,8},{11,10},{13,12},{15,14},{17,16},{19,... | collective-permute-start | bytes 1572872 | tf_op jit(solution)/shard_map/ppermute | solution.py:336
  23.5 0.0 copy-done.10
  23.5 0.0 copy-start.1
  23.5 1.0 %copy-done.1 = f32[2,256,256]{2,1,0:T(8,128)S(1)} copy-done((f32[2,256,256]{2,1,0:T(8,128)S(1)}, f32[2,256,256]{2,1,0:T(8,128)}, u32[]{:S(2)}) %copy-start.1) | copy-done | bytes 524312
  24.5 0.0 copy-start.3
  24.5 1.0 %copy-done.3 = bf16[256,768]{1,0:T(8,128)(2,1)S(1)} copy-done((bf16[256,768]{1,0:T(8,128)(2,1)S(1)}, bf16[256,768]{1,0:T(8,128)(2,1)}, u32[]{:S(2)}) %copy-start.3) | copy-done | bytes 393240
  25.5 0.0 copy-start.4
  25.5 1.0 %copy-done.4 = bf16[768,256]{1,0:T(8,128)(2,1)S(1)} copy-done((bf16[768,256]{1,0:T(8,128)(2,1)S(1)}, bf16[768,256]{1,0:T(8,128)(2,1)}, u32[]{:S(2)}) %copy-start.4) | copy-done | bytes 393240
  26.5 0.0 copy-start.5
  26.5 1.0 %copy-done.5 = bf16[768,256]{1,0:T(8,128)(2,1)S(1)} copy-done((bf16[768,256]{1,0:T(8,128)(2,1)S(1)}, bf16[768,256]{1,0:T(8,128)(2,1)}, u32[]{:S(2)}) %copy-start.5) | copy-done | bytes 393240
  27.5 0.0 copy-start.6
  27.5 1.0 %copy-done.6 = bf16[256,768]{1,0:T(8,128)(2,1)S(1)} copy-done((bf16[256,768]{1,0:T(8,128)(2,1)S(1)}, bf16[256,768]{1,0:T(8,128)(2,1)}, u32[]{:S(2)}) %copy-start.6) | copy-done | bytes 393240
  28.5 0.0 copy-start.7
  28.5 1.0 %copy-done.7 = bf16[256,768]{1,0:T(8,128)(2,1)S(1)} copy-done((bf16[256,768]{1,0:T(8,128)(2,1)S(1)}, bf16[256,768]{1,0:T(8,128)(2,1)}, u32[]{:S(2)}) %copy-start.7) | copy-done | bytes 393240
  29.5 0.0 copy-start.8
  29.5 1.0 %copy-done.8 = bf16[768,256]{1,0:T(8,128)(2,1)S(1)} copy-done((bf16[768,256]{1,0:T(8,128)(2,1)S(1)}, bf16[768,256]{1,0:T(8,128)(2,1)}, u32[]{:S(2)}) %copy-start.8) | copy-done | bytes 393240
  30.5 0.0 copy-start.9
  30.5 0.9 copy-done.9
  31.4 0.0 copy-start.2
  31.4 0.9 prepare.1
  32.3 0.0 collective-permute-done.right_ref
  32.3 0.0 collective-permute-done.2.corner_ref
  32.3 0.0 collective-permute-done.3.relayed_ref
  32.3 0.0 copy-start.11
  32.4 0.0 copy-start.12
  32.4 0.0 copy-done
  32.4 0.1 copy-done.2
  32.4 0.6 copy-done.11
  33.0 0.0 copy-done.12
  33.0 8.0 %process_scans.1 = (f32[2,256,256]{2,1,0:T(8,128)S(1)}, f32[2,256,256]{2,1,0:T(8,128)S(1)}, f32[2,256,256]{2,1,0:T(8,128)S(1)}, f32[2,256,256]{2,1,0:T(8,128)S(1...) custom-call(s32[2]{0:T(128)S(1)} %copy-done.11, s32[2]{0:T(128)S(1)} %copy-done.12, ...), custom_call_target="tpu_custom_call" | custom-call | tf_op jit(solution)/shard_map/process_scans/pallas_call | solution.py:307
  41.0 1.2 %collective-permute-start.7 = (f32[2,256,256]{2,1,0:T(8,128)S(1)}, f32[2,256,256]{2,1,0:T(8,128)S(1)}, u32[]{:S(2)}, u32[]{:S(2)}) collective-permute-start(f32[2,256,256]{2,1,0:T(8,128)S(1)} %get-tuple-element.27), channel_id=1, source_target_pairs={{0,1},{1,0},{2,3},{3,2},{4,5},{5,4},{6,7},{7,6},{8,9},{9,8},{10,11... | collective-permute-start | bytes 1572872 | tf_op jit(solution)/shard_map/ppermute | solution.py:25
  42.3 1.5 %collective-permute-done.7 = f32[2,256,256]{2,1,0:T(8,128)S(1)} collective-permute-done((f32[2,256,256]{2,1,0:T(8,128)S(1)}, f32[2,256,256]{2,1,0:T(8,128)S(1)}, u32[]{:S(2)}, u32[]{:S(2)}) %collective-permute-start.7) | collective-permute-done | bytes 524320 | tf_op jit(solution)/shard_map/ppermute | solution.py:25
  43.8 0.1 add.26
  43.9 12.8 %all_to_all.10 = f32[8,64,256]{2,1,0:T(8,128)S(1)} all-to-all(f32[8,64,256]{2,1,0:T(8,128)S(1)} %bitcast.5), channel_id=1, replica_groups={{0,2,8,10,16,18,24,26},{1,3,9,11,17,19,25,27},{4,6,12,14,20,22,28,30},{..., dimensions={0} | all-to-all | bytes 1048576 | tf_op jit(solution)/shard_map/all_to_all | solution.py:45
  56.7 1.4 %collective-permute-start.8 = (f32[64,256]{1,0:T(8,128)S(1)}, f32[64,256]{1,0:T(8,128)S(1)}, u32[]{:S(2)}, u32[]{:S(2)}) collective-permute-start(f32[64,256]{1,0:T(8,128)S(1)} %reduce_sum.9), channel_id=1, source_target_pairs={{0,4},{1,5},{2,6},{3,7},{4,0},{5,1},{6,2},{7,3},{8,12},{9,13},{10,... | collective-permute-start | bytes 196616 | tf_op jit(solution)/shard_map/ppermute | solution.py:25
  58.2 3.9 %collective-permute-done.8 = f32[64,256]{1,0:T(8,128)S(1)} collective-permute-done((f32[64,256]{1,0:T(8,128)S(1)}, f32[64,256]{1,0:T(8,128)S(1)}, u32[]{:S(2)}, u32[]{:S(2)}) %collective-permute-start.8) | collective-permute-done | bytes 65568 | tf_op jit(solution)/shard_map/ppermute | solution.py:25
  62.1 0.8 broadcast_in_dim.17
  62.9 4.9 %all-to-all-start.1 = ((f32[8,64,256]{2,1,0:T(8,128)}), f32[8,64,256]{2,1,0:T(8,128)S(1)}, u32[]{:S(2)}, u32[]{:S(2)}) async-start(f32[8,64,256]{2,1,0:T(8,128)} %broadcast_in_dim.17), calls=%async_computation.1 | async-start | bytes 1048576 | tf_op jit(solution)/shard_map/all_to_all | solution.py:51
  67.8 1.9 %collective-permute-start.5 = (f32[2,256,256]{2,1,0:T(8,128)S(1)}, f32[2,256,256]{2,1,0:T(8,128)S(1)}, u32[]{:S(2)}, u32[]{:S(2)}) collective-permute-start(f32[2,256,256]{2,1,0:T(8,128)S(1)} %get-tuple-element.25), channel_id=1, source_target_pairs={{0,1},{1,2},{2,3},{3,4},{4,5},{5,6},{6,7},{8,9},{9,10},{10,11},{11... | collective-permute-start | bytes 1572872 | tf_op jit(solution)/shard_map/ppermute | solution.py:21
  69.7 3.5 %collective-permute-start.4 = (f32[2,256,256]{2,1,0:T(8,128)S(1)}, f32[2,256,256]{2,1,0:T(8,128)S(1)}, u32[]{:S(2)}, u32[]{:S(2)}) collective-permute-start(f32[2,256,256]{2,1,0:T(8,128)S(1)} %get-tuple-element.23), channel_id=1, source_target_pairs={{0,1},{1,2},{2,3},{3,4},{4,5},{5,6},{6,7},{8,9},{9,10},{10,11},{11... | collective-permute-start | bytes 1572872 | tf_op jit(solution)/shard_map/ppermute | solution.py:21
  73.2 5.1 %collective-permute-done.5 = f32[2,256,256]{2,1,0:T(8,128)S(1)} collective-permute-done((f32[2,256,256]{2,1,0:T(8,128)S(1)}, f32[2,256,256]{2,1,0:T(8,128)S(1)}, u32[]{:S(2)}, u32[]{:S(2)}) %collective-permute-start.5) | collective-permute-done | bytes 524320 | tf_op jit(solution)/shard_map/ppermute | solution.py:21
  78.3 0.1 add.24
  78.4 3.4 %collective-permute-start.6 = (f32[2,256,256]{2,1,0:T(8,128)S(1)}, f32[2,256,256]{2,1,0:T(8,128)S(1)}, u32[]{:S(2)}, u32[]{:S(2)}) collective-permute-start(f32[2,256,256]{2,1,0:T(8,128)S(1)} %add.24), channel_id=1, source_target_pairs={{0,8},{8,16},{16,24},{1,9},{9,17},{17,25},{2,10},{10,18},{18,26},{... | collective-permute-start | bytes 1572872 | tf_op jit(solution)/shard_map/ppermute | solution.py:21
  81.7 0.0 all-to-all-done.1
  81.8 0.1 collective-permute-start.9
  81.8 2.1 %collective-permute-done.4 = f32[2,256,256]{2,1,0:T(8,128)S(1)} collective-permute-done((f32[2,256,256]{2,1,0:T(8,128)S(1)}, f32[2,256,256]{2,1,0:T(8,128)S(1)}, u32[]{:S(2)}, u32[]{:S(2)}) %collective-permute-start.4) | collective-permute-done | bytes 524320 | tf_op jit(solution)/shard_map/ppermute | solution.py:21
  83.9 0.1 add.23
  84.0 10.5 %collective-permute-done.6 = f32[2,256,256]{2,1,0:T(8,128)S(1)} collective-permute-done((f32[2,256,256]{2,1,0:T(8,128)S(1)}, f32[2,256,256]{2,1,0:T(8,128)S(1)}, u32[]{:S(2)}, u32[]{:S(2)}) %collective-permute-start.6) | collective-permute-done | bytes 524320 | tf_op jit(solution)/shard_map/ppermute | solution.py:21
  94.4 0.9 add.25
  95.3 0.1 broadcast_in_dim.16
  95.4 0.0 collective-permute-done.9
  95.4 1.1 %bitcast_dynamic-update-slice_fusion = f32[2,2,256,256]{3,2,1,0:T(8,128)S(1)} fusion(f32[2,2,256,256]{3,2,1,0:T(8,128)S(1)} %constant_dynamic-update-slice_fusion, s32[]{:T(128)S(6)} %select_n.8, f32[2,256,256]{2,1,0:T(8,128)} %collective-permute-done.9), kind=kLoop, calls=%fused_computation | loop fusion | bytes 1048580 | tf_op jit(solution)/shard_map/jit(dynamic_update_index_in_dim)/dynamic_update_slice | solution.py:353
  96.5 0.0 copy-start.13
  96.5 1.0 copy-done.13
  (3 shorter events, 0.1 us)
Async XLA Ops:
  0.6 22.8 %copy-start.10 = (f32[2,128]{1,0:T(2,128)S(1)}, f32[2,128]{1,0:T(2,128)}, u32[]{:S(2)}) copy-start(f32[2,128]{1,0:T(2,128)} %constant.46.clone.refs_4_) | copy-start | bytes 3076
  0.6 31.7 %copy-start = (f32[2,2,256,256]{3,2,1,0:T(8,128)S(1)}, f32[2,2,256,256]{3,2,1,0:T(8,128)}, u32[]{:S(2)}) copy-start(f32[2,2,256,256]{3,2,1,0:T(8,128)} %probe_ref.1) | copy-start | bytes 3145732
  0.7 21.5 %collective-permute-start.1 = (f32[2,256,256]{2,1,0:T(8,128)}, f32[2,256,256]{2,1,0:T(8,128)S(1)}, u32[]{:S(2)}, u32[]{:S(2)}) collective-permute-start(f32[2,256,256]{2,1,0:T(8,128)} %own_ref.1), channel_id=1, source_target_pairs={{8,0},{16,8},{24,16},{9,1},{17,9},{25,17},{10,2},{18,10},{26,18},{... | collective-permute-start | bytes 1572872 | tf_op jit(solution)/shard_map/ppermute | solution.py:21
  4.1 28.2 %collective-permute-start = (f32[2,256,256]{2,1,0:T(8,128)}, f32[2,256,256]{2,1,0:T(8,128)S(1)}, u32[]{:S(2)}, u32[]{:S(2)}) collective-permute-start(f32[2,256,256]{2,1,0:T(8,128)} %own_ref.1), channel_id=1, source_target_pairs={{1,0},{2,1},{3,2},{4,3},{5,4},{6,5},{7,6},{9,8},{10,9},{11,10},{12... | collective-permute-start | bytes 1572872 | tf_op jit(solution)/shard_map/ppermute | solution.py:21
  6.1 26.3 %collective-permute-start.2 = (f32[2,256,256]{2,1,0:T(8,128)}, f32[2,256,256]{2,1,0:T(8,128)S(1)}, u32[]{:S(2)}, u32[]{:S(2)}) collective-permute-start(f32[2,256,256]{2,1,0:T(8,128)} %own_ref.1), channel_id=1, source_target_pairs={{10,1},{12,3},{14,5},{18,9},{20,11},{22,13},{26,17},{28,19},{30,21}} | collective-permute-start | bytes 1572872 | tf_op jit(solution)/shard_map/ppermute | solution.py:331
  22.2 10.2 %collective-permute-start.3 = (f32[2,256,256]{2,1,0:T(8,128)S(1)}, f32[2,256,256]{2,1,0:T(8,128)S(1)}, u32[]{:S(2)}, u32[]{:S(2)}) collective-permute-start(f32[2,256,256]{2,1,0:T(8,128)S(1)} %collective-permute-done.1.below_ref), channel_id=1, source_target_pairs={{1,0},{3,2},{5,4},{7,6},{9,8},{11,10},{13,12},{15,14},{17,16},{19,... | collective-permute-start | bytes 1572872 | tf_op jit(solution)/shard_map/ppermute | solution.py:336
  23.5 1.0 %copy-start.1 = (f32[2,256,256]{2,1,0:T(8,128)S(1)}, f32[2,256,256]{2,1,0:T(8,128)}, u32[]{:S(2)}) copy-start(f32[2,256,256]{2,1,0:T(8,128)} %measured_ref.1) | copy-start | bytes 1572868
  24.5 1.0 %copy-start.3 = (bf16[256,768]{1,0:T(8,128)(2,1)S(1)}, bf16[256,768]{1,0:T(8,128)(2,1)}, u32[]{:S(2)}) copy-start(bf16[256,768]{1,0:T(8,128)(2,1)} %constant.40.clone.pick_rows_ref) | copy-start | bytes 1179652
  25.5 1.0 %copy-start.4 = (bf16[768,256]{1,0:T(8,128)(2,1)S(1)}, bf16[768,256]{1,0:T(8,128)(2,1)}, u32[]{:S(2)}) copy-start(bf16[768,256]{1,0:T(8,128)(2,1)} %constant.41.clone.pick_cols_ref) | copy-start | bytes 1179652
  26.5 1.0 %copy-start.5 = (bf16[768,256]{1,0:T(8,128)(2,1)S(1)}, bf16[768,256]{1,0:T(8,128)(2,1)}, u32[]{:S(2)}) copy-start(bf16[768,256]{1,0:T(8,128)(2,1)} %constant.42.clone.refs_0_) | copy-start | bytes 1179652
  27.5 1.0 %copy-start.6 = (bf16[256,768]{1,0:T(8,128)(2,1)S(1)}, bf16[256,768]{1,0:T(8,128)(2,1)}, u32[]{:S(2)}) copy-start(bf16[256,768]{1,0:T(8,128)(2,1)} %constant.43.clone.refs_1_) | copy-start | bytes 1179652
  28.5 1.0 %copy-start.7 = (bf16[256,768]{1,0:T(8,128)(2,1)S(1)}, bf16[256,768]{1,0:T(8,128)(2,1)}, u32[]{:S(2)}) copy-start(bf16[256,768]{1,0:T(8,128)(2,1)} %constant.44.clone.refs_2_) | copy-start | bytes 1179652
  29.5 1.0 %copy-start.8 = (bf16[768,256]{1,0:T(8,128)(2,1)S(1)}, bf16[768,256]{1,0:T(8,128)(2,1)}, u32[]{:S(2)}) copy-start(bf16[768,256]{1,0:T(8,128)(2,1)} %constant.45.clone.refs_3_) | copy-start | bytes 1179652
  30.5 0.9 copy-start.9
  31.4 1.0 %copy-start.2 = (f32[2,256,256]{2,1,0:T(8,128)S(1)}, f32[2,256,256]{2,1,0:T(8,128)}, u32[]{:S(2)}) copy-start(f32[2,256,256]{2,1,0:T(8,128)} %own_ref.1) | copy-start | bytes 1572868
  32.3 0.7 copy-start.11
  32.4 0.7 copy-start.12
  41.0 2.8 %collective-permute-start.7 = (f32[2,256,256]{2,1,0:T(8,128)S(1)}, f32[2,256,256]{2,1,0:T(8,128)S(1)}, u32[]{:S(2)}, u32[]{:S(2)}) collective-permute-start(f32[2,256,256]{2,1,0:T(8,128)S(1)} %get-tuple-element.27), channel_id=1, source_target_pairs={{0,1},{1,0},{2,3},{3,2},{4,5},{5,4},{6,7},{7,6},{8,9},{9,8},{10,11... | collective-permute-start | bytes 1572872 | tf_op jit(solution)/shard_map/ppermute | solution.py:25
  56.7 5.3 %collective-permute-start.8 = (f32[64,256]{1,0:T(8,128)S(1)}, f32[64,256]{1,0:T(8,128)S(1)}, u32[]{:S(2)}, u32[]{:S(2)}) collective-permute-start(f32[64,256]{1,0:T(8,128)S(1)} %reduce_sum.9), channel_id=1, source_target_pairs={{0,4},{1,5},{2,6},{3,7},{4,0},{5,1},{6,2},{7,3},{8,12},{9,13},{10,... | collective-permute-start | bytes 196616 | tf_op jit(solution)/shard_map/ppermute | solution.py:25
  62.9 18.8 %all-to-all-start.1 = ((f32[8,64,256]{2,1,0:T(8,128)}), f32[8,64,256]{2,1,0:T(8,128)S(1)}, u32[]{:S(2)}, u32[]{:S(2)}) async-start(f32[8,64,256]{2,1,0:T(8,128)} %broadcast_in_dim.17), calls=%async_computation.1 | async-start | bytes 1048576 | tf_op jit(solution)/shard_map/all_to_all | solution.py:51
  67.8 10.5 %collective-permute-start.5 = (f32[2,256,256]{2,1,0:T(8,128)S(1)}, f32[2,256,256]{2,1,0:T(8,128)S(1)}, u32[]{:S(2)}, u32[]{:S(2)}) collective-permute-start(f32[2,256,256]{2,1,0:T(8,128)S(1)} %get-tuple-element.25), channel_id=1, source_target_pairs={{0,1},{1,2},{2,3},{3,4},{4,5},{5,6},{6,7},{8,9},{9,10},{10,11},{11... | collective-permute-start | bytes 1572872 | tf_op jit(solution)/shard_map/ppermute | solution.py:21
  69.7 14.2 %collective-permute-start.4 = (f32[2,256,256]{2,1,0:T(8,128)S(1)}, f32[2,256,256]{2,1,0:T(8,128)S(1)}, u32[]{:S(2)}, u32[]{:S(2)}) collective-permute-start(f32[2,256,256]{2,1,0:T(8,128)S(1)} %get-tuple-element.23), channel_id=1, source_target_pairs={{0,1},{1,2},{2,3},{3,4},{4,5},{5,6},{6,7},{8,9},{9,10},{10,11},{11... | collective-permute-start | bytes 1572872 | tf_op jit(solution)/shard_map/ppermute | solution.py:21
  78.4 16.1 %collective-permute-start.6 = (f32[2,256,256]{2,1,0:T(8,128)S(1)}, f32[2,256,256]{2,1,0:T(8,128)S(1)}, u32[]{:S(2)}, u32[]{:S(2)}) collective-permute-start(f32[2,256,256]{2,1,0:T(8,128)S(1)} %add.24), channel_id=1, source_target_pairs={{0,8},{8,16},{16,24},{1,9},{9,17},{17,25},{2,10},{10,18},{18,26},{... | collective-permute-start | bytes 1572872 | tf_op jit(solution)/shard_map/ppermute | solution.py:21
  81.8 13.7 %collective-permute-start.9 = (f32[2,256,256]{2,1,0:T(8,128)S(1)}, f32[2,256,256]{2,1,0:T(8,128)}, u32[]{:S(2)}, u32[]{:S(2)}) collective-permute-start(f32[2,256,256]{2,1,0:T(8,128)S(1)} %bitcast.6), channel_id=1, source_target_pairs={{0,1},{1,0},{2,3},{3,2},{4,5},{5,4},{6,7},{7,6},{8,9},{9,8},{10,11... | collective-permute-start | bytes 1572872 | tf_op jit(solution)/shard_map/ppermute | solution.py:25
  96.5 1.0 copy-start.13
where the time goes:
time: 98.2 us; the launch traced here: 97.5 us
  waiting for transfers between devices  36.7 us (37%)
  starting transfers between devices  25.5 us (26%)
  blocking collectives  12.8 us (13%)
  local copies, waits for them, and re-layouts  11.6 us (12%)
  Pallas kernels  8.91 us (9%)
  other arithmetic  1.14 us (1%)
    ppermute x5, waiting for transfers between devices, shifted(): return lax.ppermute(block, axis, route)  31.2 us
    ppermute x5, starting transfers between devices, shifted(): return lax.ppermute(block, axis, route)  14.2 us
    all_to_all x1, blocking collectives, scatter_sum(): lax.all_to_all(pieces, ('row', 'col'), 0, 0, axis_index_groups=groups)  12.8 us
    unnamed x28, local copies, waits for them, and re-layouts  9.55 us
    pallas_call x1, Pallas kernels, process_scans(): pl.pallas_call(scan_kernel, out_shape=[VMEM(shape, jnp.float32) for shape...  8 us
    ppermute x3, waiting for transfers between devices, swapped(): lax.ppermute(block, axis, [(i, i ^ mask) for i in range(lax.axis_size(axi...  5.44 us
    all_to_all x1, starting transfers between devices, gather_slices(): lax.all_to_all(copies, ('row', 'col'), 0, 0, axis_index_groups=groups)  4.88 us
    ppermute x3, starting transfers between devices, swapped(): lax.ppermute(block, axis, [(i, i ^ mask) for i in range(lax.axis_size(axi...  2.7 us
  transfers between devices with their start and end apart: 11, of which 6 were waited for; matrix products, arithmetic and copies ran while one was open for 1% of the time, Pallas kernels for 1%

commit v1 on v0

--- a/solution.py
+++ b/solution.py
@@ -1,3 +1,4 @@
+import functools
 import math
 
 import jax
@@ -133,8 +134,10 @@
     across_ref,
     own_ref,
     right_ref,
-    below_ref,
-    corner_ref,
+    below_first_ref,
+    below_last_ref,
+    corner_first_ref,
+    corner_last_ref,
     relayed_ref,
     probe_ref,
     measured_ref,
@@ -179,9 +182,12 @@
         back_across = lax.rem(length - across, length)
         patch = []
         for part in range(2):
+            below = jnp.concatenate([below_first_ref[part], below_last_ref[part]], axis=0)
+            corner_last = corner_last_ref[part] + relayed_ref[part]
+            corner = jnp.concatenate([corner_first_ref[part], corner_last], axis=0)
             merged = jnp.where(
                 later_row,
-                jnp.where(later_col, corner_ref[part] + relayed_ref[part], below_ref[part]),
+                jnp.where(later_col, corner, below),
                 jnp.where(later_col, right_ref[part], own_ref[part]),
             )
             patch.append(pltpu.roll(pltpu.roll(merged, up, 0), back_across, 1))
@@ -279,8 +285,8 @@
                     out[part] = out[part] + piece
 
 
-def in_vmem(*arrays):
-    return [pltpu.with_memory_space_constraint(array, VMEM) for array in arrays]
+def in_space(space, *arrays):
+    return [pltpu.with_memory_space_constraint(array, space) for array in arrays]
 
 
 def whole():
@@ -297,12 +303,12 @@
         out_specs=[whole()] * (1 + len(consts)),
         compiler_params=pltpu.CompilerParams(vmem_limit_bytes=PREPARE_VMEM),
         name="prepare",
-    )(measured, *picks, *consts)
+    )(*in_space(pltpu.HBM, measured, *picks, *consts))
 
 
 def process_scans(offsets, tiles, probe_modes, measured, consts):
     modes, _, length, _ = probe_modes.shape
-    operands = in_vmem(*tiles, probe_modes, measured, *consts)
+    operands = in_space(VMEM, *tiles, probe_modes, measured, *consts)
     results = [tiles[0].shape] * 4 + [probe_modes.shape[1:]] * 2
     return pl.pallas_call(
         scan_kernel,
@@ -315,6 +321,46 @@
     )(*offsets, *operands)
 
 
+def place_kernel(step, values_ref, *refs):
+    out_ref, sem = refs[-2], refs[-1]
+    mode = lax.rem(lax.axis_index("col"), 2) ^ step
+    copy = pltpu.make_async_copy(values_ref, out_ref.at[mode], sem)
+    copy.start()
+    copy.wait()
+
+
+def place_mode(values, modes, step, into=None):
+    before = () if into is None else (into,)
+    return pl.pallas_call(
+        functools.partial(place_kernel, step),
+        out_shape=jax.ShapeDtypeStruct((modes,) + values.shape, values.dtype),
+        in_specs=[whole()] + [pl.BlockSpec(memory_space=pl.ANY)] * len(before),
+        out_specs=pl.BlockSpec(memory_space=pl.ANY),
+        scratch_shapes=[pltpu.SemaphoreType.DMA],
+        input_output_aliases={1: 0} if before else {},
+        compiler_params=pltpu.CompilerParams(vmem_limit_bytes=PREPARE_VMEM),
+        name="place_mode",
+    )(*in_space(VMEM, values), *before)
+
+
+def add_kernel(*refs):
+    total = refs[0][...]
+    for ref in refs[1:-1]:
+        total = total + ref[...]
+    refs[-1][...] = total
+
+
+def add_tiles(*tiles, out):
+    return pl.pallas_call(
+        add_kernel,
+        out_shape=out,
+        in_specs=[whole()] * len(tiles),
+        out_specs=whole(),
+        compiler_params=pltpu.CompilerParams(vmem_limit_bytes=PREPARE_VMEM),
+        name="add_tiles",
+    )(*in_space(VMEM, *tiles))
+
+
 def on_device(transmission, probe_modes, measured, offset_down, offset_across):
     length = probe_modes.shape[-1]
     scan_count = measured.shape[0]
@@ -322,22 +368,31 @@
     core = lax.rem(lax.axis_index("col"), 2)
     table = tables(length)
 
-    below = shifted(transmission, "row", -1)
+    middle = transmission.shape[1] // 2
+    first, rest = lax.optimization_barrier((transmission[:, :middle], transmission))
+    last = rest[:, middle:]
     direct = [
         ((row + 1) * cols + col + 1, row * cols + col)
         for row in range(rows - 1)
         for col in range(1, cols - 1, 2)
     ]
-    corner = lax.ppermute(transmission, ("row", "col"), direct)
+    below_first = shifted(first, "row", -1)
+    below_last = shifted(last, "row", -1)
     right = shifted(transmission, "col", -1)
+    corner_last = lax.ppermute(last, ("row", "col"), direct)
+    corner_first = shifted(below_first, "col", -1)
     consts = [table[name] for name in ("right_f", "left_f", "left_b", "right_b", "lane", "sub")]
     picks = [table["pick_rows"], table["pick_cols"]]
     *consts, ordered = prepare(measured, picks, consts)
-    relayed = lax.ppermute(below, "col", [(col + 1, col) for col in range(0, cols - 1, 2)])
+    relayed = lax.ppermute(below_last, "col", [(col + 1, col) for col in range(0, cols - 1, 2)])
 
     offsets = (offset_down, offset_across)
     own, to_right, to_below, to_corner, keep, send = process_scans(
-        offsets, (transmission, right, below, corner, relayed), probe_modes, ordered, consts
+        offsets,
+        (transmission, right, below_first, below_last, corner_first, corner_last, relayed),
+        probe_modes,
+        ordered,
+        consts,
     )
 
     keep = keep + swapped(send, "col", 1)
@@ -348,13 +403,16 @@
     scans_total = scan_count * rows * cols
     mine = gather_slices(piece * (1.0 / math.sqrt(scans_total)), groups).reshape(keep.shape)
     other = swapped(mine, "col", 1)
-    probe_gradient = jnp.zeros(probe_modes.shape, jnp.float32)
-    probe_gradient = lax.dynamic_update_index_in_dim(probe_gradient, mine, core, 0)
-    probe_gradient = lax.dynamic_update_index_in_dim(probe_gradient, other, 1 - core, 0)
-
-    to_below = to_below + shifted(to_corner, "col", 1)
-    own = lax.optimization_barrier(own + shifted(to_right, "col", 1))
-    own = own + shifted(to_below, "row", 1)
+    probe_gradient = place_mode(mine, probe_modes.shape[0], 0)
+    probe_gradient = place_mode(other, probe_modes.shape[0], 1, probe_gradient)
+
+    relayed = lax.ppermute(to_corner, "col", [(col, col + 1) for col in range(0, cols - 1, 2)])
+    to_below = add_tiles(to_below, relayed, out=VMEM(to_below.shape, jnp.float32))
+    from_left = shifted(to_right, "col", 1)
+    from_above = shifted(to_below, "row", 1)
+    from_corner = lax.ppermute(to_corner, ("row", "col"), [(end, start) for start, end in direct])
+    tile = jax.ShapeDtypeStruct(own.shape, jnp.float32)
+    own = add_tiles(own, from_left, from_above, from_corner, out=tile)
     return own, probe_gradient
 
 

time: 98.2 us -> 90 us (0.916)
  the two profiles are of different devices: /device:TPU:20 before, /device:TPU:13 now
where the time goes in v1:
time: 90 us; the launch traced here: 89.5 us
  starting transfers between devices  35 us (39%)
  waiting for transfers between devices  24.4 us (27%)
  Pallas kernels  14.2 us (16%)
  blocking collectives  12.4 us (14%)
  local copies, waits for them, and re-layouts  2.65 us (3%)
    ppermute x6, waiting for transfers between devices, shifted(): return lax.ppermute(block, axis, route)  19.8 us
    ppermute x6, starting transfers between devices, shifted(): return lax.ppermute(block, axis, route)  15.8 us
    all_to_all x1, blocking collectives, scatter_sum(): lax.all_to_all(pieces, ('row', 'col'), 0, 0, axis_index_groups=groups)  12.4 us
    pallas_call x1, Pallas kernels, process_scans(): pl.pallas_call(scan_kernel, out_shape=[VMEM(shape, jnp.float32) for shape...  8.93 us
    ppermute x1, starting transfers between devices, on_device(): lax.ppermute(to_corner, ('row', 'col'), [(end, start) for start, end in d...  6.23 us
    ppermute x3, waiting for transfers between devices, swapped(): lax.ppermute(block, axis, [(i, i ^ mask) for i in range(lax.axis_size(axi...  4.63 us
    all_to_all x1, starting transfers between devices, gather_slices(): lax.all_to_all(copies, ('row', 'col'), 0, 0, axis_index_groups=groups)  4.51 us
    ppermute x1, starting transfers between devices, on_device(): lax.ppermute(below_last, 'col', [(col + 1, col) for col in range(0, cols...  3.95 us
  transfers between devices with their start and end apart: 14, of which 6 were waited for; matrix products, arithmetic and copies ran while one was open for 0% of the time, Pallas kernels for 5%

profile of v1, /device:TPU:13, one launch (start us, length us, event | category | flops | bytes accessed | tf_op | source)
XLA Modules:
  0.0 89.5 jit_solution(5272456614035154868)
XLA Ops:
  0.6 0.0 copy-start
  0.6 1.0 %slice.6 = f32[2,128,256]{2,1,0:T(8,128)S(1)} slice(f32[2,256,256]{2,1,0:T(8,128)} %own_ref.1), slice={[0:2], [0:128], [0:256]} | slice | bytes 524288 | tf_op jit(solution)/shard_map/slice | solution.py:372
  1.7 0.1 copy-done
  1.8 0.0 copy-start.1
  1.8 3.2 %collective-permute-start.2 = (f32[2,128,256]{2,1,0:T(8,128)S(1)}, f32[2,128,256]{2,1,0:T(8,128)S(1)}, u32[]{:S(2)}, u32[]{:S(2)}) collective-permute-start(f32[2,128,256]{2,1,0:T(8,128)S(1)} %slice.7), channel_id=1, source_target_pairs={{8,0},{16,8},{24,16},{9,1},{17,9},{25,17},{10,2},{18,10},{26,18},{... | collective-permute-start | bytes 786440 | tf_op jit(solution)/shard_map/ppermute | solution.py:22
  5.0 2.2 %collective-permute-start.1 = (f32[2,128,256]{2,1,0:T(8,128)S(1)}, f32[2,128,256]{2,1,0:T(8,128)S(1)}, u32[]{:S(2)}, u32[]{:S(2)}) collective-permute-start(f32[2,128,256]{2,1,0:T(8,128)S(1)} %slice.6), channel_id=1, source_target_pairs={{8,0},{16,8},{24,16},{9,1},{17,9},{25,17},{10,2},{18,10},{26,18},{... | collective-permute-start | bytes 786440 | tf_op jit(solution)/shard_map/ppermute | solution.py:22
  7.2 3.1 %collective-permute-start = (f32[2,256,256]{2,1,0:T(8,128)S(1)}, f32[2,256,256]{2,1,0:T(8,128)S(1)}, u32[]{:S(2)}, u32[]{:S(2)}) collective-permute-start(f32[2,256,256]{2,1,0:T(8,128)S(1)} %copy-done), channel_id=1, source_target_pairs={{1,0},{2,1},{3,2},{4,3},{5,4},{6,5},{7,6},{9,8},{10,9},{11,10},{12... | collective-permute-start | bytes 1572872 | tf_op jit(solution)/shard_map/ppermute | solution.py:22
  10.3 1.3 %collective-permute-start.4 = (f32[2,128,256]{2,1,0:T(8,128)S(1)}, f32[2,128,256]{2,1,0:T(8,128)S(1)}, u32[]{:S(2)}, u32[]{:S(2)}) collective-permute-start(f32[2,128,256]{2,1,0:T(8,128)S(1)} %slice.7), channel_id=1, source_target_pairs={{10,1},{12,3},{14,5},{18,9},{20,11},{22,13},{26,17},{28,19},{30,21}} | collective-permute-start | bytes 786440 | tf_op jit(solution)/shard_map/ppermute | solution.py:382
  11.6 0.0 collective-permute-done.2.below_last_ref
  11.6 4.0 %collective-permute-start.5 = (f32[2,128,256]{2,1,0:T(8,128)S(1)}, f32[2,128,256]{2,1,0:T(8,128)S(1)}, u32[]{:S(2)}, u32[]{:S(2)}) collective-permute-start(f32[2,128,256]{2,1,0:T(8,128)S(1)} %collective-permute-done.2.below_last_ref), channel_id=1, source_target_pairs={{1,0},{3,2},{5,4},{7,6},{9,8},{11,10},{13,12},{15,14},{17,16},{19,... | collective-permute-start | bytes 786440 | tf_op jit(solution)/shard_map/ppermute | solution.py:387
  15.6 1.0 %collective-permute-done.1.below_first_ref = f32[2,128,256]{2,1,0:T(8,128)S(1)} collective-permute-done((f32[2,128,256]{2,1,0:T(8,128)S(1)}, f32[2,128,256]{2,1,0:T(8,128)S(1)}, u32[]{:S(2)}, u32[]{:S(2)}) %collective-permute-start.1) | collective-permute-done | bytes 262176 | tf_op jit(solution)/shard_map/ppermute | solution.py:22
  16.6 3.4 %collective-permute-start.3 = (f32[2,128,256]{2,1,0:T(8,128)S(1)}, f32[2,128,256]{2,1,0:T(8,128)S(1)}, u32[]{:S(2)}, u32[]{:S(2)}) collective-permute-start(f32[2,128,256]{2,1,0:T(8,128)S(1)} %collective-permute-done.1.below_first_ref), channel_id=1, source_target_pairs={{1,0},{2,1},{3,2},{4,3},{5,4},{6,5},{7,6},{9,8},{10,9},{11,10},{12... | collective-permute-start | bytes 786440 | tf_op jit(solution)/shard_map/ppermute | solution.py:22
  20.1 2.7 %prepare.1 = (bf16[768,256]{1,0:T(8,128)(2,1)S(1)}, bf16[256,768]{1,0:T(8,128)(2,1)S(1)}, bf16[256,768]{1,0:T(8,128)(2,1)S(1)}, bf16[768,256]{1,0:T(8,128)(2,1)S...) custom-call(f32[2,256,256]{2,1,0:T(8,128)} %measured_ref.1, ...), custom_call_target="tpu_custom_call" | custom-call | tf_op jit(solution)/shard_map/prepare/pallas_call | solution.py:299
  22.8 0.0 collective-permute-done.4.corner_last_ref
  22.8 0.0 collective-permute-done.5.relayed_ref
  22.8 2.5 %collective-permute-done.3.corner_first_ref = f32[2,128,256]{2,1,0:T(8,128)S(1)} collective-permute-done((f32[2,128,256]{2,1,0:T(8,128)S(1)}, f32[2,128,256]{2,1,0:T(8,128)S(1)}, u32[]{:S(2)}, u32[]{:S(2)}) %collective-permute-start.3) | collective-permute-done | bytes 262176 | tf_op jit(solution)/shard_map/ppermute | solution.py:22
  25.3 0.0 collective-permute-done.right_ref
  25.3 0.0 copy-start.2
  25.3 0.0 copy-start.3
  25.3 0.0 copy-done.1
  25.3 0.6 copy-done.2
  25.9 0.0 copy-done.3
  26.0 8.9 %process_scans.1 = (f32[2,256,256]{2,1,0:T(8,128)S(1)}, f32[2,256,256]{2,1,0:T(8,128)}, f32[2,256,256]{2,1,0:T(8,128)S(1)}, f32[2,256,256]{2,1,0:T(8,128)}, f32[...) custom-call(s32[2]{0:T(128)S(1)} %copy-done.2, s32[2]{0:T(128)S(1)} %copy-done.3, f32[2,256,256]{2,1,0:T(8,128)S(1)} %copy-done, ...), custom_call_target="tpu_custom_call" | custom-call | tf_op jit(solution)/shard_map/process_scans/pallas_call | solution.py:313
  34.9 0.0 collective-permute-start.10
  34.9 1.9 %collective-permute-done.10 = f32[2,256,256]{2,1,0:T(8,128)S(1)} collective-permute-done((f32[2,256,256]{2,1,0:T(8,128)S(1)}, f32[2,256,256]{2,1,0:T(8,128)S(1)}, u32[]{:S(2)}, u32[]{:S(2)}) %collective-permute-start.10) | collective-permute-done | bytes 524320 | tf_op jit(solution)/shard_map/ppermute | solution.py:26
  36.8 0.1 add.6
  36.9 12.4 %all_to_all.10 = f32[8,64,256]{2,1,0:T(8,128)S(1)} all-to-all(f32[8,64,256]{2,1,0:T(8,128)S(1)} %bitcast.4), channel_id=1, replica_groups={{0,2,8,10,16,18,24,26},{1,3,9,11,17,19,25,27},{4,6,12,14,20,22,28,30},{..., dimensions={0} | all-to-all | bytes 1048576 | tf_op jit(solution)/shard_map/all_to_all | solution.py:46
  49.3 1.4 %collective-permute-start.11 = (f32[64,256]{1,0:T(8,128)S(1)}, f32[64,256]{1,0:T(8,128)S(1)}, u32[]{:S(2)}, u32[]{:S(2)}) collective-permute-start(f32[64,256]{1,0:T(8,128)S(1)} %reduce_sum.9), channel_id=1, source_target_pairs={{0,4},{1,5},{2,6},{3,7},{4,0},{5,1},{6,2},{7,3},{8,12},{9,13},{10,... | collective-permute-start | bytes 196616 | tf_op jit(solution)/shard_map/ppermute | solution.py:26
  50.6 2.7 %collective-permute-done.11 = f32[64,256]{1,0:T(8,128)S(1)} collective-permute-done((f32[64,256]{1,0:T(8,128)S(1)}, f32[64,256]{1,0:T(8,128)S(1)}, u32[]{:S(2)}, u32[]{:S(2)}) %collective-permute-start.11) | collective-permute-done | bytes 65568 | tf_op jit(solution)/shard_map/ppermute | solution.py:26
  53.4 0.8 broadcast_in_dim.2
  54.2 4.5 %all-to-all-start.1 = ((f32[8,64,256]{2,1,0:T(8,128)}), f32[8,64,256]{2,1,0:T(8,128)S(1)}, u32[]{:S(2)}, u32[]{:S(2)}) async-start(f32[8,64,256]{2,1,0:T(8,128)} %broadcast_in_dim.2), calls=%async_computation.1 | async-start | bytes 1048576 | tf_op jit(solution)/shard_map/all_to_all | solution.py:52
  58.7 1.3 %collective-permute-start.7 = (f32[2,256,256]{2,1,0:T(8,128)}, f32[2,256,256]{2,1,0:T(8,128)S(1)}, u32[]{:S(2)}, u32[]{:S(2)}) collective-permute-start(f32[2,256,256]{2,1,0:T(8,128)} %get-tuple-element.29), channel_id=1, source_target_pairs={{0,1},{2,3},{4,5},{6,7},{8,9},{10,11},{12,13},{14,15},{16,17},{18,... | collective-permute-start | bytes 1572872 | tf_op jit(solution)/shard_map/ppermute | solution.py:409
  60.0 6.2 %collective-permute-start.9 = (f32[2,256,256]{2,1,0:T(8,128)}, f32[2,256,256]{2,1,0:T(8,128)S(1)}, u32[]{:S(2)}, u32[]{:S(2)}) collective-permute-start(f32[2,256,256]{2,1,0:T(8,128)} %get-tuple-element.29), channel_id=1, source_target_pairs={{1,10},{3,12},{5,14},{9,18},{11,20},{13,22},{17,26},{19,28},{21,30}} | collective-permute-start | bytes 1572872 | tf_op jit(solution)/shard_map/ppermute | solution.py:413
  66.3 1.9 %collective-permute-start.6 = (f32[2,256,256]{2,1,0:T(8,128)}, f32[2,256,256]{2,1,0:T(8,128)S(1)}, u32[]{:S(2)}, u32[]{:S(2)}) collective-permute-start(f32[2,256,256]{2,1,0:T(8,128)} %get-tuple-element.27), channel_id=1, source_target_pairs={{0,1},{1,2},{2,3},{3,4},{4,5},{5,6},{6,7},{8,9},{9,10},{10,11},{11... | collective-permute-start | bytes 1572872 | tf_op jit(solution)/shard_map/ppermute | solution.py:22
  68.2 0.0 collective-permute-done.7.refs_1_
  68.2 0.1 add_tiles.2
  68.3 1.9 %collective-permute-start.8 = (f32[2,256,256]{2,1,0:T(8,128)S(1)}, f32[2,256,256]{2,1,0:T(8,128)S(1)}, u32[]{:S(2)}, u32[]{:S(2)}) collective-permute-start(f32[2,256,256]{2,1,0:T(8,128)S(1)} %add_tiles.2), channel_id=1, source_target_pairs={{0,8},{8,16},{16,24},{1,9},{9,17},{17,25},{2,10},{10,18},{18,26},{... | collective-permute-start | bytes 1572872 | tf_op jit(solution)/shard_map/ppermute | solution.py:22
  70.2 0.0 all-to-all-done.1
  70.2 0.6 collective-permute-start.12
  70.8 7.5 %collective-permute-done.6.refs_1_ = f32[2,256,256]{2,1,0:T(8,128)S(1)} collective-permute-done((f32[2,256,256]{2,1,0:T(8,128)}, f32[2,256,256]{2,1,0:T(8,128)S(1)}, u32[]{:S(2)}, u32[]{:S(2)}) %collective-permute-start.6) | collective-permute-done | bytes 524320 | tf_op jit(solution)/shard_map/ppermute | solution.py:22
  78.3 0.0 collective-permute-done.9.refs_3_
  78.3 8.7 %collective-permute-done.8.refs_2_ = f32[2,256,256]{2,1,0:T(8,128)S(1)} collective-permute-done((f32[2,256,256]{2,1,0:T(8,128)S(1)}, f32[2,256,256]{2,1,0:T(8,128)S(1)}, u32[]{:S(2)}, u32[]{:S(2)}) %collective-permute-start.8) | collective-permute-done | bytes 524320 | tf_op jit(solution)/shard_map/ppermute | solution.py:22
  87.0 0.9 add_tiles.3
  87.9 0.8 place_mode.2.refs_0_
  88.7 0.0 collective-permute-done.12.values_ref
  88.7 0.8 place_mode.3
  (3 shorter events, 0.1 us)
Async XLA Ops:
  0.6 1.1 %copy-start = (f32[2,256,256]{2,1,0:T(8,128)S(1)}, f32[2,256,256]{2,1,0:T(8,128)}, u32[]{:S(2)}) copy-start(f32[2,256,256]{2,1,0:T(8,128)} %own_ref.1) | copy-start | bytes 1572868
  1.8 23.5 %copy-start.1 = (f32[2,2,256,256]{3,2,1,0:T(8,128)S(1)}, f32[2,2,256,256]{3,2,1,0:T(8,128)}, u32[]{:S(2)}) copy-start(f32[2,2,256,256]{3,2,1,0:T(8,128)} %probe_ref.1) | copy-start | bytes 3145732
  1.8 9.8 %collective-permute-start.2 = (f32[2,128,256]{2,1,0:T(8,128)S(1)}, f32[2,128,256]{2,1,0:T(8,128)S(1)}, u32[]{:S(2)}, u32[]{:S(2)}) collective-permute-start(f32[2,128,256]{2,1,0:T(8,128)S(1)} %slice.7), channel_id=1, source_target_pairs={{8,0},{16,8},{24,16},{9,1},{17,9},{25,17},{10,2},{18,10},{26,18},{... | collective-permute-start | bytes 786440 | tf_op jit(solution)/shard_map/ppermute | solution.py:22
  5.0 11.6 %collective-permute-start.1 = (f32[2,128,256]{2,1,0:T(8,128)S(1)}, f32[2,128,256]{2,1,0:T(8,128)S(1)}, u32[]{:S(2)}, u32[]{:S(2)}) collective-permute-start(f32[2,128,256]{2,1,0:T(8,128)S(1)} %slice.6), channel_id=1, source_target_pairs={{8,0},{16,8},{24,16},{9,1},{17,9},{25,17},{10,2},{18,10},{26,18},{... | collective-permute-start | bytes 786440 | tf_op jit(solution)/shard_map/ppermute | solution.py:22
  7.2 18.1 %collective-permute-start = (f32[2,256,256]{2,1,0:T(8,128)S(1)}, f32[2,256,256]{2,1,0:T(8,128)S(1)}, u32[]{:S(2)}, u32[]{:S(2)}) collective-permute-start(f32[2,256,256]{2,1,0:T(8,128)S(1)} %copy-done), channel_id=1, source_target_pairs={{1,0},{2,1},{3,2},{4,3},{5,4},{6,5},{7,6},{9,8},{10,9},{11,10},{12... | collective-permute-start | bytes 1572872 | tf_op jit(solution)/shard_map/ppermute | solution.py:22
  10.3 12.5 %collective-permute-start.4 = (f32[2,128,256]{2,1,0:T(8,128)S(1)}, f32[2,128,256]{2,1,0:T(8,128)S(1)}, u32[]{:S(2)}, u32[]{:S(2)}) collective-permute-start(f32[2,128,256]{2,1,0:T(8,128)S(1)} %slice.7), channel_id=1, source_target_pairs={{10,1},{12,3},{14,5},{18,9},{20,11},{22,13},{26,17},{28,19},{30,21}} | collective-permute-start | bytes 786440 | tf_op jit(solution)/shard_map/ppermute | solution.py:382
  11.6 11.2 %collective-permute-start.5 = (f32[2,128,256]{2,1,0:T(8,128)S(1)}, f32[2,128,256]{2,1,0:T(8,128)S(1)}, u32[]{:S(2)}, u32[]{:S(2)}) collective-permute-start(f32[2,128,256]{2,1,0:T(8,128)S(1)} %collective-permute-done.2.below_last_ref), channel_id=1, source_target_pairs={{1,0},{3,2},{5,4},{7,6},{9,8},{11,10},{13,12},{15,14},{17,16},{19,... | collective-permute-start | bytes 786440 | tf_op jit(solution)/shard_map/ppermute | solution.py:387
  16.6 8.7 %collective-permute-start.3 = (f32[2,128,256]{2,1,0:T(8,128)S(1)}, f32[2,128,256]{2,1,0:T(8,128)S(1)}, u32[]{:S(2)}, u32[]{:S(2)}) collective-permute-start(f32[2,128,256]{2,1,0:T(8,128)S(1)} %collective-permute-done.1.below_first_ref), channel_id=1, source_target_pairs={{1,0},{2,1},{3,2},{4,3},{5,4},{6,5},{7,6},{9,8},{10,9},{11,10},{12... | collective-permute-start | bytes 786440 | tf_op jit(solution)/shard_map/ppermute | solution.py:22
  25.3 0.7 copy-start.2
  25.3 0.7 copy-start.3
  34.9 1.9 %collective-permute-start.10 = (f32[2,256,256]{2,1,0:T(8,128)S(1)}, f32[2,256,256]{2,1,0:T(8,128)S(1)}, u32[]{:S(2)}, u32[]{:S(2)}) collective-permute-start(f32[2,256,256]{2,1,0:T(8,128)S(1)} %get-tuple-element.31), channel_id=1, source_target_pairs={{0,1},{1,0},{2,3},{3,2},{4,5},{5,4},{6,7},{7,6},{8,9},{9,8},{10,11... | collective-permute-start | bytes 1572872 | tf_op jit(solution)/shard_map/ppermute | solution.py:26
  49.3 4.1 %collective-permute-start.11 = (f32[64,256]{1,0:T(8,128)S(1)}, f32[64,256]{1,0:T(8,128)S(1)}, u32[]{:S(2)}, u32[]{:S(2)}) collective-permute-start(f32[64,256]{1,0:T(8,128)S(1)} %reduce_sum.9), channel_id=1, source_target_pairs={{0,4},{1,5},{2,6},{3,7},{4,0},{5,1},{6,2},{7,3},{8,12},{9,13},{10,... | collective-permute-start | bytes 196616 | tf_op jit(solution)/shard_map/ppermute | solution.py:26
  54.2 16.0 %all-to-all-start.1 = ((f32[8,64,256]{2,1,0:T(8,128)}), f32[8,64,256]{2,1,0:T(8,128)S(1)}, u32[]{:S(2)}, u32[]{:S(2)}) async-start(f32[8,64,256]{2,1,0:T(8,128)} %broadcast_in_dim.2), calls=%async_computation.1 | async-start | bytes 1048576 | tf_op jit(solution)/shard_map/all_to_all | solution.py:52
  58.7 9.5 %collective-permute-start.7 = (f32[2,256,256]{2,1,0:T(8,128)}, f32[2,256,256]{2,1,0:T(8,128)S(1)}, u32[]{:S(2)}, u32[]{:S(2)}) collective-permute-start(f32[2,256,256]{2,1,0:T(8,128)} %get-tuple-element.29), channel_id=1, source_target_pairs={{0,1},{2,3},{4,5},{6,7},{8,9},{10,11},{12,13},{14,15},{16,17},{18,... | collective-permute-start | bytes 1572872 | tf_op jit(solution)/shard_map/ppermute | solution.py:409
  60.0 18.3 %collective-permute-start.9 = (f32[2,256,256]{2,1,0:T(8,128)}, f32[2,256,256]{2,1,0:T(8,128)S(1)}, u32[]{:S(2)}, u32[]{:S(2)}) collective-permute-start(f32[2,256,256]{2,1,0:T(8,128)} %get-tuple-element.29), channel_id=1, source_target_pairs={{1,10},{3,12},{5,14},{9,18},{11,20},{13,22},{17,26},{19,28},{21,30}} | collective-permute-start | bytes 1572872 | tf_op jit(solution)/shard_map/ppermute | solution.py:413
  66.3 12.1 %collective-permute-start.6 = (f32[2,256,256]{2,1,0:T(8,128)}, f32[2,256,256]{2,1,0:T(8,128)S(1)}, u32[]{:S(2)}, u32[]{:S(2)}) collective-permute-start(f32[2,256,256]{2,1,0:T(8,128)} %get-tuple-element.27), channel_id=1, source_target_pairs={{0,1},{1,2},{2,3},{3,4},{4,5},{5,6},{6,7},{8,9},{9,10},{10,11},{11... | collective-permute-start | bytes 1572872 | tf_op jit(solution)/shard_map/ppermute | solution.py:22
  68.3 18.7 %collective-permute-start.8 = (f32[2,256,256]{2,1,0:T(8,128)S(1)}, f32[2,256,256]{2,1,0:T(8,128)S(1)}, u32[]{:S(2)}, u32[]{:S(2)}) collective-permute-start(f32[2,256,256]{2,1,0:T(8,128)S(1)} %add_tiles.2), channel_id=1, source_target_pairs={{0,8},{8,16},{16,24},{1,9},{9,17},{17,25},{2,10},{10,18},{18,26},{... | collective-permute-start | bytes 1572872 | tf_op jit(solution)/shard_map/ppermute | solution.py:22
  70.2 18.5 %collective-permute-start.12 = (f32[2,256,256]{2,1,0:T(8,128)S(1)}, f32[2,256,256]{2,1,0:T(8,128)S(1)}, u32[]{:S(2)}, u32[]{:S(2)}) collective-permute-start(f32[2,256,256]{2,1,0:T(8,128)S(1)} %bitcast.2), channel_id=1, source_target_pairs={{0,1},{1,0},{2,3},{3,2},{4,5},{5,4},{6,7},{7,6},{8,9},{9,8},{10,11... | collective-permute-start | bytes 1572872 | tf_op jit(solution)/shard_map/ppermute | solution.py:26

commit v2 on v1

--- a/solution.py
+++ b/solution.py
@@ -318,7 +318,7 @@
         scratch_shapes=[VMEM((modes, length, 2 * length), jnp.float32)],
         compiler_params=pltpu.CompilerParams(vmem_limit_bytes=PROCESS_VMEM),
         name="process_scans",
-    )(*offsets, *operands)
+    )(*in_space(SMEM, *offsets), *operands)
 
 
 def place_kernel(step, values_ref, *refs):
@@ -406,13 +406,26 @@
     probe_gradient = place_mode(mine, probe_modes.shape[0], 0)
     probe_gradient = place_mode(other, probe_modes.shape[0], 1, probe_gradient)
 
-    relayed = lax.ppermute(to_corner, "col", [(col, col + 1) for col in range(0, cols - 1, 2)])
-    to_below = add_tiles(to_below, relayed, out=VMEM(to_below.shape, jnp.float32))
+    def across(cores):
+        return [(col, col + 1) for col in range(cores, cols - 1, 2)]
+
+    def downward(cores):
+        return [
+            (row * cols + col, (row + 1) * cols + col)
+            for row in range(rows - 1)
+            for col in range(cores, cols, 2)
+        ]
+
+    tile = jax.ShapeDtypeStruct(own.shape, jnp.float32)
+    on_chip = VMEM(own.shape, jnp.float32)
+    relayed = lax.ppermute(to_corner, "col", across(0))
+    passed = lax.ppermute(to_corner, "col", across(1))
+    to_below_odd = add_tiles(to_below, relayed, out=on_chip)
+    above_odd = lax.ppermute(to_below_odd, ("row", "col"), downward(1))
+    to_below_even = add_tiles(to_below, passed, out=on_chip)
+    above_even = lax.ppermute(to_below_even, ("row", "col"), downward(0))
     from_left = shifted(to_right, "col", 1)
-    from_above = shifted(to_below, "row", 1)
-    from_corner = lax.ppermute(to_corner, ("row", "col"), [(end, start) for start, end in direct])
-    tile = jax.ShapeDtypeStruct(own.shape, jnp.float32)
-    own = add_tiles(own, from_left, from_above, from_corner, out=tile)
+    own = add_tiles(own, from_left, above_odd, above_even, out=tile)
     return own, probe_gradient
 
 

time: 90 us -> 91.8 us (1.020); the launches traced: 89.5 us -> 90 us
  waiting for transfers between devices: 24.4 us -> 18.4 us
  starting transfers between devices: 35 us -> 40.6 us
    ppermute x6 -> x5, waiting for transfers between devices: 19.8 us -> 3.53 us  [shifted(): return lax.ppermute(block, axis, route)]
    ppermute x2 -> x4, waiting for transfers between devices: 0.01 us -> 10.2 us  [the longest x1 9.27 us: on_device(): above_odd = lax.ppermute(to_below_odd, ('row', 'col'), downward(1))]
    ppermute x2 -> x4, starting transfers between devices: 7.51 us -> 10.4 us  [the longest x1 5.28 us: on_device(): passed = lax.ppermute(to_corner, 'col', across(1))]
    ppermute x3, starting transfers between devices: 1.93 us -> 4.46 us  [swapped(): lax.ppermute(block, axis, [(i, i ^ mask) for i in range(lax.axis_size(axi...]
    ppermute x6 -> x5, starting transfers between devices: 15.8 us -> 16.1 us  [shifted(): return lax.ppermute(block, axis, route)]
  transfers between devices with their start and end apart: 14 -> 15, of which waited for: 6 -> 6; matrix products, arithmetic and copies ran while one was open for 0% -> 0% of each run, Pallas kernels for 5% -> 6%
where the time goes in v2:
time: 91.8 us; the launch traced here: 90 us
  starting transfers between devices  40.6 us (44%)
  waiting for transfers between devices  18.4 us (20%)
  Pallas kernels  15 us (16%)
  blocking collectives  12.4 us (14%)
  local copies, waits for them, and re-layouts  2.64 us (3%)
    ppermute x5, starting transfers between devices, shifted(): return lax.ppermute(block, axis, route)  16.1 us
    all_to_all x1, blocking collectives, scatter_sum(): lax.all_to_all(pieces, ('row', 'col'), 0, 0, axis_index_groups=groups)  12.4 us
    ppermute x1, waiting for transfers between devices, on_device(): above_odd = lax.ppermute(to_below_odd, ('row', 'col'), downward(1))  9.27 us
    pallas_call x1, Pallas kernels, process_scans(): pl.pallas_call(scan_kernel, out_shape=[VMEM(shape, jnp.float32) for shape...  8.93 us
    ppermute x1, starting transfers between devices, on_device(): passed = lax.ppermute(to_corner, 'col', across(1))  5.28 us
    ppermute x3, waiting for transfers between devices, swapped(): lax.ppermute(block, axis, [(i, i ^ mask) for i in range(lax.axis_size(axi...  4.63 us
    all_to_all x1, starting transfers between devices, gather_slices(): lax.all_to_all(copies, ('row', 'col'), 0, 0, axis_index_groups=groups)  4.51 us
    ppermute x3, starting transfers between devices, swapped(): lax.ppermute(block, axis, [(i, i ^ mask) for i in range(lax.axis_size(axi...  4.46 us
  transfers between devices with their start and end apart: 15, of which 6 were waited for; matrix products, arithmetic and copies ran while one was open for 0% of the time, Pallas kernels for 6%

profile of v2, /device:TPU:13, one launch (start us, length us, event | category | flops | bytes accessed | tf_op | source)
XLA Modules:
  0.0 90.0 jit_solution(14078959757981854517)
XLA Ops:
  0.6 0.0 copy-start
  0.6 1.0 %slice.6 = f32[2,128,256]{2,1,0:T(8,128)S(1)} slice(f32[2,256,256]{2,1,0:T(8,128)} %own_ref.1), slice={[0:2], [0:128], [0:256]} | slice | bytes 524288 | tf_op jit(solution)/shard_map/slice | solution.py:372
  1.7 0.1 copy-done
  1.8 0.0 copy-start.1
  1.8 3.2 %collective-permute-start.2 = (f32[2,128,256]{2,1,0:T(8,128)S(1)}, f32[2,128,256]{2,1,0:T(8,128)S(1)}, u32[]{:S(2)}, u32[]{:S(2)}) collective-permute-start(f32[2,128,256]{2,1,0:T(8,128)S(1)} %slice.7), channel_id=1, source_target_pairs={{8,0},{16,8},{24,16},{9,1},{17,9},{25,17},{10,2},{18,10},{26,18},{... | collective-permute-start | bytes 786440 | tf_op jit(solution)/shard_map/ppermute | solution.py:22
  5.0 2.2 %collective-permute-start.1 = (f32[2,128,256]{2,1,0:T(8,128)S(1)}, f32[2,128,256]{2,1,0:T(8,128)S(1)}, u32[]{:S(2)}, u32[]{:S(2)}) collective-permute-start(f32[2,128,256]{2,1,0:T(8,128)S(1)} %slice.6), channel_id=1, source_target_pairs={{8,0},{16,8},{24,16},{9,1},{17,9},{25,17},{10,2},{18,10},{26,18},{... | collective-permute-start | bytes 786440 | tf_op jit(solution)/shard_map/ppermute | solution.py:22
  7.2 3.1 %collective-permute-start = (f32[2,256,256]{2,1,0:T(8,128)S(1)}, f32[2,256,256]{2,1,0:T(8,128)S(1)}, u32[]{:S(2)}, u32[]{:S(2)}) collective-permute-start(f32[2,256,256]{2,1,0:T(8,128)S(1)} %copy-done), channel_id=1, source_target_pairs={{1,0},{2,1},{3,2},{4,3},{5,4},{6,5},{7,6},{9,8},{10,9},{11,10},{12... | collective-permute-start | bytes 1572872 | tf_op jit(solution)/shard_map/ppermute | solution.py:22
  10.3 1.3 %collective-permute-start.4 = (f32[2,128,256]{2,1,0:T(8,128)S(1)}, f32[2,128,256]{2,1,0:T(8,128)S(1)}, u32[]{:S(2)}, u32[]{:S(2)}) collective-permute-start(f32[2,128,256]{2,1,0:T(8,128)S(1)} %slice.7), channel_id=1, source_target_pairs={{10,1},{12,3},{14,5},{18,9},{20,11},{22,13},{26,17},{28,19},{30,21}} | collective-permute-start | bytes 786440 | tf_op jit(solution)/shard_map/ppermute | solution.py:382
  11.6 0.0 collective-permute-done.2.below_last_ref
  11.6 4.0 %collective-permute-start.5 = (f32[2,128,256]{2,1,0:T(8,128)S(1)}, f32[2,128,256]{2,1,0:T(8,128)S(1)}, u32[]{:S(2)}, u32[]{:S(2)}) collective-permute-start(f32[2,128,256]{2,1,0:T(8,128)S(1)} %collective-permute-done.2.below_last_ref), channel_id=1, source_target_pairs={{1,0},{3,2},{5,4},{7,6},{9,8},{11,10},{13,12},{15,14},{17,16},{19,... | collective-permute-start | bytes 786440 | tf_op jit(solution)/shard_map/ppermute | solution.py:387
  15.6 1.0 %collective-permute-done.1.below_first_ref = f32[2,128,256]{2,1,0:T(8,128)S(1)} collective-permute-done((f32[2,128,256]{2,1,0:T(8,128)S(1)}, f32[2,128,256]{2,1,0:T(8,128)S(1)}, u32[]{:S(2)}, u32[]{:S(2)}) %collective-permute-start.1) | collective-permute-done | bytes 262176 | tf_op jit(solution)/shard_map/ppermute | solution.py:22
  16.6 3.4 %collective-permute-start.3 = (f32[2,128,256]{2,1,0:T(8,128)S(1)}, f32[2,128,256]{2,1,0:T(8,128)S(1)}, u32[]{:S(2)}, u32[]{:S(2)}) collective-permute-start(f32[2,128,256]{2,1,0:T(8,128)S(1)} %collective-permute-done.1.below_first_ref), channel_id=1, source_target_pairs={{1,0},{2,1},{3,2},{4,3},{5,4},{6,5},{7,6},{9,8},{10,9},{11,10},{12... | collective-permute-start | bytes 786440 | tf_op jit(solution)/shard_map/ppermute | solution.py:22
  20.1 2.7 %prepare.1 = (bf16[768,256]{1,0:T(8,128)(2,1)S(1)}, bf16[256,768]{1,0:T(8,128)(2,1)S(1)}, bf16[256,768]{1,0:T(8,128)(2,1)S(1)}, bf16[768,256]{1,0:T(8,128)(2,1)S...) custom-call(f32[2,256,256]{2,1,0:T(8,128)} %measured_ref.1, ...), custom_call_target="tpu_custom_call" | custom-call | tf_op jit(solution)/shard_map/prepare/pallas_call | solution.py:299
  22.8 0.0 collective-permute-done.4.corner_last_ref
  22.8 0.0 collective-permute-done.5.relayed_ref
  22.8 2.5 %collective-permute-done.3.corner_first_ref = f32[2,128,256]{2,1,0:T(8,128)S(1)} collective-permute-done((f32[2,128,256]{2,1,0:T(8,128)S(1)}, f32[2,128,256]{2,1,0:T(8,128)S(1)}, u32[]{:S(2)}, u32[]{:S(2)}) %collective-permute-start.3) | collective-permute-done | bytes 262176 | tf_op jit(solution)/shard_map/ppermute | solution.py:22
  25.3 0.0 collective-permute-done.right_ref
  25.3 0.0 copy-start.2
  25.3 0.0 copy-start.3
  25.3 0.0 copy-done.1
  25.3 0.6 copy-done.2
  25.9 0.0 copy-done.3
  26.0 8.9 %process_scans.1 = (f32[2,256,256]{2,1,0:T(8,128)S(1)}, f32[2,256,256]{2,1,0:T(8,128)}, f32[2,256,256]{2,1,0:T(8,128)S(1)}, f32[2,256,256]{2,1,0:T(8,128)}, f32[...) custom-call(s32[2]{0:T(128)S(1)} %copy-done.2, s32[2]{0:T(128)S(1)} %copy-done.3, f32[2,256,256]{2,1,0:T(8,128)S(1)} %copy-done, ...), custom_call_target="tpu_custom_call" | custom-call | tf_op jit(solution)/shard_map/process_scans/pallas_call | solution.py:313
  34.9 0.0 collective-permute-start.11
  34.9 1.9 %collective-permute-done.11 = f32[2,256,256]{2,1,0:T(8,128)S(1)} collective-permute-done((f32[2,256,256]{2,1,0:T(8,128)S(1)}, f32[2,256,256]{2,1,0:T(8,128)S(1)}, u32[]{:S(2)}, u32[]{:S(2)}) %collective-permute-start.11) | collective-permute-done | bytes 524320 | tf_op jit(solution)/shard_map/ppermute | solution.py:26
  36.8 0.1 add.6
  36.9 12.4 %all_to_all.10 = f32[8,64,256]{2,1,0:T(8,128)S(1)} all-to-all(f32[8,64,256]{2,1,0:T(8,128)S(1)} %bitcast.4), channel_id=1, replica_groups={{0,2,8,10,16,18,24,26},{1,3,9,11,17,19,25,27},{4,6,12,14,20,22,28,30},{..., dimensions={0} | all-to-all | bytes 1048576 | tf_op jit(solution)/shard_map/all_to_all | solution.py:46
  49.3 1.4 %collective-permute-start.12 = (f32[64,256]{1,0:T(8,128)S(1)}, f32[64,256]{1,0:T(8,128)S(1)}, u32[]{:S(2)}, u32[]{:S(2)}) collective-permute-start(f32[64,256]{1,0:T(8,128)S(1)} %reduce_sum.9), channel_id=1, source_target_pairs={{0,4},{1,5},{2,6},{3,7},{4,0},{5,1},{6,2},{7,3},{8,12},{9,13},{10,... | collective-permute-start | bytes 196616 | tf_op jit(solution)/shard_map/ppermute | solution.py:26
  50.7 2.7 %collective-permute-done.12 = f32[64,256]{1,0:T(8,128)S(1)} collective-permute-done((f32[64,256]{1,0:T(8,128)S(1)}, f32[64,256]{1,0:T(8,128)S(1)}, u32[]{:S(2)}, u32[]{:S(2)}) %collective-permute-start.12) | collective-permute-done | bytes 65568 | tf_op jit(solution)/shard_map/ppermute | solution.py:26
  53.4 0.8 broadcast_in_dim.2
  54.2 4.5 %all-to-all-start.1 = ((f32[8,64,256]{2,1,0:T(8,128)}), f32[8,64,256]{2,1,0:T(8,128)S(1)}, u32[]{:S(2)}, u32[]{:S(2)}) async-start(f32[8,64,256]{2,1,0:T(8,128)} %broadcast_in_dim.2), calls=%async_computation.1 | async-start | bytes 1048576 | tf_op jit(solution)/shard_map/all_to_all | solution.py:52
  58.7 5.3 %collective-permute-start.9 = (f32[2,256,256]{2,1,0:T(8,128)}, f32[2,256,256]{2,1,0:T(8,128)S(1)}, u32[]{:S(2)}, u32[]{:S(2)}) collective-permute-start(f32[2,256,256]{2,1,0:T(8,128)} %get-tuple-element.29), channel_id=1, source_target_pairs={{1,2},{3,4},{5,6},{9,10},{11,12},{13,14},{17,18},{19,20},{21,22},{... | collective-permute-start | bytes 1572872 | tf_op jit(solution)/shard_map/ppermute | solution.py:422
  64.0 1.3 %collective-permute-start.7 = (f32[2,256,256]{2,1,0:T(8,128)}, f32[2,256,256]{2,1,0:T(8,128)S(1)}, u32[]{:S(2)}, u32[]{:S(2)}) collective-permute-start(f32[2,256,256]{2,1,0:T(8,128)} %get-tuple-element.29), channel_id=1, source_target_pairs={{0,1},{2,3},{4,5},{6,7},{8,9},{10,11},{12,13},{14,15},{16,17},{18,... | collective-permute-start | bytes 1572872 | tf_op jit(solution)/shard_map/ppermute | solution.py:421
  65.3 4.1 %collective-permute-start.6 = (f32[2,256,256]{2,1,0:T(8,128)}, f32[2,256,256]{2,1,0:T(8,128)S(1)}, u32[]{:S(2)}, u32[]{:S(2)}) collective-permute-start(f32[2,256,256]{2,1,0:T(8,128)} %get-tuple-element.27), channel_id=1, source_target_pairs={{0,1},{1,2},{2,3},{3,4},{4,5},{5,6},{6,7},{8,9},{9,10},{10,11},{11... | collective-permute-start | bytes 1572872 | tf_op jit(solution)/shard_map/ppermute | solution.py:22
  69.5 0.9 %collective-permute-done.9.refs_1_ = f32[2,256,256]{2,1,0:T(8,128)S(1)} collective-permute-done((f32[2,256,256]{2,1,0:T(8,128)}, f32[2,256,256]{2,1,0:T(8,128)S(1)}, u32[]{:S(2)}, u32[]{:S(2)}) %collective-permute-start.9) | collective-permute-done | bytes 524320 | tf_op jit(solution)/shard_map/ppermute | solution.py:422
  70.4 0.1 add_tiles.4
  70.5 0.7 collective-permute-start.10
  71.2 0.0 collective-permute-done.7.refs_1_
  71.2 0.8 add_tiles.3
  72.0 3.1 %collective-permute-start.8 = (f32[2,256,256]{2,1,0:T(8,128)}, f32[2,256,256]{2,1,0:T(8,128)S(1)}, u32[]{:S(2)}, u32[]{:S(2)}) collective-permute-start(f32[2,256,256]{2,1,0:T(8,128)} %add_tiles.3), channel_id=1, source_target_pairs={{1,9},{3,11},{5,13},{7,15},{9,17},{11,19},{13,21},{15,23},{17,25},... | collective-permute-start | bytes 1572872 | tf_op jit(solution)/shard_map/ppermute | solution.py:424
  75.1 0.0 all-to-all-done.1
  75.2 3.1 %collective-permute-start.13 = (f32[2,256,256]{2,1,0:T(8,128)S(1)}, f32[2,256,256]{2,1,0:T(8,128)S(1)}, u32[]{:S(2)}, u32[]{:S(2)}) collective-permute-start(f32[2,256,256]{2,1,0:T(8,128)S(1)} %bitcast.2), channel_id=1, source_target_pairs={{0,1},{1,0},{2,3},{3,2},{4,5},{5,4},{6,7},{7,6},{8,9},{9,8},{10,11... | collective-permute-start | bytes 1572872 | tf_op jit(solution)/shard_map/ppermute | solution.py:26
  78.2 0.0 collective-permute-done.6.refs_1_
  78.3 0.0 collective-permute-done.10.refs_3_
  78.3 9.3 %collective-permute-done.8.refs_2_ = f32[2,256,256]{2,1,0:T(8,128)S(1)} collective-permute-done((f32[2,256,256]{2,1,0:T(8,128)}, f32[2,256,256]{2,1,0:T(8,128)S(1)}, u32[]{:S(2)}, u32[]{:S(2)}) %collective-permute-start.8) | collective-permute-done | bytes 524320 | tf_op jit(solution)/shard_map/ppermute | solution.py:424
  87.5 0.9 add_tiles.5
  88.4 0.8 place_mode.2.refs_0_
  89.2 0.0 collective-permute-done.13.values_ref
  89.2 0.8 place_mode.3
  (3 shorter events, 0.1 us)
Async XLA Ops:
  0.6 1.1 %copy-start = (f32[2,256,256]{2,1,0:T(8,128)S(1)}, f32[2,256,256]{2,1,0:T(8,128)}, u32[]{:S(2)}) copy-start(f32[2,256,256]{2,1,0:T(8,128)} %own_ref.1) | copy-start | bytes 1572868
  1.8 23.5 %copy-start.1 = (f32[2,2,256,256]{3,2,1,0:T(8,128)S(1)}, f32[2,2,256,256]{3,2,1,0:T(8,128)}, u32[]{:S(2)}) copy-start(f32[2,2,256,256]{3,2,1,0:T(8,128)} %probe_ref.1) | copy-start | bytes 3145732
  1.8 9.8 %collective-permute-start.2 = (f32[2,128,256]{2,1,0:T(8,128)S(1)}, f32[2,128,256]{2,1,0:T(8,128)S(1)}, u32[]{:S(2)}, u32[]{:S(2)}) collective-permute-start(f32[2,128,256]{2,1,0:T(8,128)S(1)} %slice.7), channel_id=1, source_target_pairs={{8,0},{16,8},{24,16},{9,1},{17,9},{25,17},{10,2},{18,10},{26,18},{... | collective-permute-start | bytes 786440 | tf_op jit(solution)/shard_map/ppermute | solution.py:22
  5.0 11.6 %collective-permute-start.1 = (f32[2,128,256]{2,1,0:T(8,128)S(1)}, f32[2,128,256]{2,1,0:T(8,128)S(1)}, u32[]{:S(2)}, u32[]{:S(2)}) collective-permute-start(f32[2,128,256]{2,1,0:T(8,128)S(1)} %slice.6), channel_id=1, source_target_pairs={{8,0},{16,8},{24,16},{9,1},{17,9},{25,17},{10,2},{18,10},{26,18},{... | collective-permute-start | bytes 786440 | tf_op jit(solution)/shard_map/ppermute | solution.py:22
  7.2 18.1 %collective-permute-start = (f32[2,256,256]{2,1,0:T(8,128)S(1)}, f32[2,256,256]{2,1,0:T(8,128)S(1)}, u32[]{:S(2)}, u32[]{:S(2)}) collective-permute-start(f32[2,256,256]{2,1,0:T(8,128)S(1)} %copy-done), channel_id=1, source_target_pairs={{1,0},{2,1},{3,2},{4,3},{5,4},{6,5},{7,6},{9,8},{10,9},{11,10},{12... | collective-permute-start | bytes 1572872 | tf_op jit(solution)/shard_map/ppermute | solution.py:22
  10.3 12.5 %collective-permute-start.4 = (f32[2,128,256]{2,1,0:T(8,128)S(1)}, f32[2,128,256]{2,1,0:T(8,128)S(1)}, u32[]{:S(2)}, u32[]{:S(2)}) collective-permute-start(f32[2,128,256]{2,1,0:T(8,128)S(1)} %slice.7), channel_id=1, source_target_pairs={{10,1},{12,3},{14,5},{18,9},{20,11},{22,13},{26,17},{28,19},{30,21}} | collective-permute-start | bytes 786440 | tf_op jit(solution)/shard_map/ppermute | solution.py:382
  11.6 11.2 %collective-permute-start.5 = (f32[2,128,256]{2,1,0:T(8,128)S(1)}, f32[2,128,256]{2,1,0:T(8,128)S(1)}, u32[]{:S(2)}, u32[]{:S(2)}) collective-permute-start(f32[2,128,256]{2,1,0:T(8,128)S(1)} %collective-permute-done.2.below_last_ref), channel_id=1, source_target_pairs={{1,0},{3,2},{5,4},{7,6},{9,8},{11,10},{13,12},{15,14},{17,16},{19,... | collective-permute-start | bytes 786440 | tf_op jit(solution)/shard_map/ppermute | solution.py:387
  16.6 8.7 %collective-permute-start.3 = (f32[2,128,256]{2,1,0:T(8,128)S(1)}, f32[2,128,256]{2,1,0:T(8,128)S(1)}, u32[]{:S(2)}, u32[]{:S(2)}) collective-permute-start(f32[2,128,256]{2,1,0:T(8,128)S(1)} %collective-permute-done.1.below_first_ref), channel_id=1, source_target_pairs={{1,0},{2,1},{3,2},{4,3},{5,4},{6,5},{7,6},{9,8},{10,9},{11,10},{12... | collective-permute-start | bytes 786440 | tf_op jit(solution)/shard_map/ppermute | solution.py:22
  25.3 0.7 copy-start.2
  25.3 0.7 copy-start.3
  34.9 1.9 %collective-permute-start.11 = (f32[2,256,256]{2,1,0:T(8,128)S(1)}, f32[2,256,256]{2,1,0:T(8,128)S(1)}, u32[]{:S(2)}, u32[]{:S(2)}) collective-permute-start(f32[2,256,256]{2,1,0:T(8,128)S(1)} %get-tuple-element.31), channel_id=1, source_target_pairs={{0,1},{1,0},{2,3},{3,2},{4,5},{5,4},{6,7},{7,6},{8,9},{9,8},{10,11... | collective-permute-start | bytes 1572872 | tf_op jit(solution)/shard_map/ppermute | solution.py:26
  49.3 4.1 %collective-permute-start.12 = (f32[64,256]{1,0:T(8,128)S(1)}, f32[64,256]{1,0:T(8,128)S(1)}, u32[]{:S(2)}, u32[]{:S(2)}) collective-permute-start(f32[64,256]{1,0:T(8,128)S(1)} %reduce_sum.9), channel_id=1, source_target_pairs={{0,4},{1,5},{2,6},{3,7},{4,0},{5,1},{6,2},{7,3},{8,12},{9,13},{10,... | collective-permute-start | bytes 196616 | tf_op jit(solution)/shard_map/ppermute | solution.py:26
  54.2 20.9 %all-to-all-start.1 = ((f32[8,64,256]{2,1,0:T(8,128)}), f32[8,64,256]{2,1,0:T(8,128)S(1)}, u32[]{:S(2)}, u32[]{:S(2)}) async-start(f32[8,64,256]{2,1,0:T(8,128)} %broadcast_in_dim.2), calls=%async_computation.1 | async-start | bytes 1048576 | tf_op jit(solution)/shard_map/all_to_all | solution.py:52
  58.7 11.7 %collective-permute-start.9 = (f32[2,256,256]{2,1,0:T(8,128)}, f32[2,256,256]{2,1,0:T(8,128)S(1)}, u32[]{:S(2)}, u32[]{:S(2)}) collective-permute-start(f32[2,256,256]{2,1,0:T(8,128)} %get-tuple-element.29), channel_id=1, source_target_pairs={{1,2},{3,4},{5,6},{9,10},{11,12},{13,14},{17,18},{19,20},{21,22},{... | collective-permute-start | bytes 1572872 | tf_op jit(solution)/shard_map/ppermute | solution.py:422
  64.0 7.2 %collective-permute-start.7 = (f32[2,256,256]{2,1,0:T(8,128)}, f32[2,256,256]{2,1,0:T(8,128)S(1)}, u32[]{:S(2)}, u32[]{:S(2)}) collective-permute-start(f32[2,256,256]{2,1,0:T(8,128)} %get-tuple-element.29), channel_id=1, source_target_pairs={{0,1},{2,3},{4,5},{6,7},{8,9},{10,11},{12,13},{14,15},{16,17},{18,... | collective-permute-start | bytes 1572872 | tf_op jit(solution)/shard_map/ppermute | solution.py:421
  65.3 12.9 %collective-permute-start.6 = (f32[2,256,256]{2,1,0:T(8,128)}, f32[2,256,256]{2,1,0:T(8,128)S(1)}, u32[]{:S(2)}, u32[]{:S(2)}) collective-permute-start(f32[2,256,256]{2,1,0:T(8,128)} %get-tuple-element.27), channel_id=1, source_target_pairs={{0,1},{1,2},{2,3},{3,4},{4,5},{5,6},{6,7},{8,9},{9,10},{10,11},{11... | collective-permute-start | bytes 1572872 | tf_op jit(solution)/shard_map/ppermute | solution.py:22
  70.5 7.8 %collective-permute-start.10 = (f32[2,256,256]{2,1,0:T(8,128)S(1)}, f32[2,256,256]{2,1,0:T(8,128)S(1)}, u32[]{:S(2)}, u32[]{:S(2)}) collective-permute-start(f32[2,256,256]{2,1,0:T(8,128)S(1)} %add_tiles.4), channel_id=1, source_target_pairs={{0,8},{2,10},{4,12},{6,14},{8,16},{10,18},{12,20},{14,22},{16,24},... | collective-permute-start | bytes 1572872 | tf_op jit(solution)/shard_map/ppermute | solution.py:426
  72.0 15.5 %collective-permute-start.8 = (f32[2,256,256]{2,1,0:T(8,128)}, f32[2,256,256]{2,1,0:T(8,128)S(1)}, u32[]{:S(2)}, u32[]{:S(2)}) collective-permute-start(f32[2,256,256]{2,1,0:T(8,128)} %add_tiles.3), channel_id=1, source_target_pairs={{1,9},{3,11},{5,13},{7,15},{9,17},{11,19},{13,21},{15,23},{17,25},... | collective-permute-start | bytes 1572872 | tf_op jit(solution)/shard_map/ppermute | solution.py:424
  75.2 14.1 %collective-permute-start.13 = (f32[2,256,256]{2,1,0:T(8,128)S(1)}, f32[2,256,256]{2,1,0:T(8,128)S(1)}, u32[]{:S(2)}, u32[]{:S(2)}) collective-permute-start(f32[2,256,256]{2,1,0:T(8,128)S(1)} %bitcast.2), channel_id=1, source_target_pairs={{0,1},{1,0},{2,3},{3,2},{4,5},{5,4},{6,7},{7,6},{8,9},{9,8},{10,11... | collective-permute-start | bytes 1572872 | tf_op jit(solution)/shard_map/ppermute | solution.py:26

commit v3 on v1

--- a/solution.py
+++ b/solution.py
@@ -42,9 +42,7 @@
 def scatter_sum(values, groups):
     count = len(groups[0])
     pieces = values.reshape((count, values.shape[0] // count) + values.shape[1:])
-    return jnp.sum(
-        lax.all_to_all(pieces, ("row", "col"), 0, 0, axis_index_groups=groups), axis=0
-    )
+    return sum_pieces(lax.all_to_all(pieces, ("row", "col"), 0, 0, axis_index_groups=groups))
 
 
 def gather_slices(piece, groups):
@@ -318,7 +316,22 @@
         scratch_shapes=[VMEM((modes, length, 2 * length), jnp.float32)],
         compiler_params=pltpu.CompilerParams(vmem_limit_bytes=PROCESS_VMEM),
         name="process_scans",
-    )(*offsets, *operands)
+    )(*in_space(pltpu.HBM, *offsets), *operands)
+
+
+def sum_kernel(pieces_ref, out_ref):
+    out_ref[...] = jnp.sum(pieces_ref[...], axis=0)
+
+
+def sum_pieces(pieces):
+    return pl.pallas_call(
+        sum_kernel,
+        out_shape=VMEM(pieces.shape[1:], pieces.dtype),
+        in_specs=[whole()],
+        out_specs=whole(),
+        compiler_params=pltpu.CompilerParams(vmem_limit_bytes=PREPARE_VMEM),
+        name="sum_pieces",
+    )(*in_space(VMEM, pieces))
 
 
 def place_kernel(step, values_ref, *refs):

time: 90 us -> 89.5 us (level)
  no operation moved by 1% of the time
where the time goes in v3:
time: 89.5 us; the launch traced here: 89 us
  starting transfers between devices  34.9 us (39%)
  waiting for transfers between devices  24.4 us (27%)
  Pallas kernels  14.3 us (16%)
  blocking collectives  12.4 us (14%)
  local copies, waits for them, and re-layouts  1.98 us (2%)
    ppermute x6, waiting for transfers between devices, shifted(): return lax.ppermute(block, axis, route)  19.8 us
    ppermute x6, starting transfers between devices, shifted(): return lax.ppermute(block, axis, route)  15.8 us
    all_to_all x1, blocking collectives, scatter_sum(): lax.all_to_all(pieces, ('row', 'col'), 0, 0, axis_index_groups=groups)  12.4 us
    pallas_call x1, Pallas kernels, process_scans(): pl.pallas_call(scan_kernel, out_shape=[VMEM(shape, jnp.float32) for shape...  9.03 us
    ppermute x1, starting transfers between devices, on_device(): lax.ppermute(to_corner, ('row', 'col'), [(end, start) for start, end in d...  6.22 us
    ppermute x3, waiting for transfers between devices, swapped(): lax.ppermute(block, axis, [(i, i ^ mask) for i in range(lax.axis_size(axi...  4.64 us
    all_to_all x1, starting transfers between devices, gather_slices(): lax.all_to_all(copies, ('row', 'col'), 0, 0, axis_index_groups=groups)  4.51 us
    ppermute x1, starting transfers between devices, on_device(): lax.ppermute(below_last, 'col', [(col + 1, col) for col in range(0, cols...  3.95 us
  transfers between devices with their start and end apart: 14, of which 6 were waited for; matrix products, arithmetic and copies ran while one was open for 0% of the time, Pallas kernels for 5%

profile of v3, /device:TPU:13, one launch (start us, length us, event | category | flops | bytes accessed | tf_op | source)
XLA Modules:
  0.0 89.0 jit_solution(5037287674055487009)
XLA Ops:
  0.6 0.0 copy-start
  0.6 1.0 %slice.6 = f32[2,128,256]{2,1,0:T(8,128)S(1)} slice(f32[2,256,256]{2,1,0:T(8,128)} %own_ref.1), slice={[0:2], [0:128], [0:256]} | slice | bytes 524288 | tf_op jit(solution)/shard_map/slice | solution.py:385
  1.7 0.1 copy-done
  1.8 0.0 copy-start.1
  1.8 3.2 %collective-permute-start.2 = (f32[2,128,256]{2,1,0:T(8,128)S(1)}, f32[2,128,256]{2,1,0:T(8,128)S(1)}, u32[]{:S(2)}, u32[]{:S(2)}) collective-permute-start(f32[2,128,256]{2,1,0:T(8,128)S(1)} %slice.7), channel_id=1, source_target_pairs={{8,0},{16,8},{24,16},{9,1},{17,9},{25,17},{10,2},{18,10},{26,18},{... | collective-permute-start | bytes 786440 | tf_op jit(solution)/shard_map/ppermute | solution.py:22
  5.0 2.2 %collective-permute-start.1 = (f32[2,128,256]{2,1,0:T(8,128)S(1)}, f32[2,128,256]{2,1,0:T(8,128)S(1)}, u32[]{:S(2)}, u32[]{:S(2)}) collective-permute-start(f32[2,128,256]{2,1,0:T(8,128)S(1)} %slice.6), channel_id=1, source_target_pairs={{8,0},{16,8},{24,16},{9,1},{17,9},{25,17},{10,2},{18,10},{26,18},{... | collective-permute-start | bytes 786440 | tf_op jit(solution)/shard_map/ppermute | solution.py:22
  7.2 3.1 %collective-permute-start = (f32[2,256,256]{2,1,0:T(8,128)S(1)}, f32[2,256,256]{2,1,0:T(8,128)S(1)}, u32[]{:S(2)}, u32[]{:S(2)}) collective-permute-start(f32[2,256,256]{2,1,0:T(8,128)S(1)} %copy-done), channel_id=1, source_target_pairs={{1,0},{2,1},{3,2},{4,3},{5,4},{6,5},{7,6},{9,8},{10,9},{11,10},{12... | collective-permute-start | bytes 1572872 | tf_op jit(solution)/shard_map/ppermute | solution.py:22
  10.3 1.3 %collective-permute-start.4 = (f32[2,128,256]{2,1,0:T(8,128)S(1)}, f32[2,128,256]{2,1,0:T(8,128)S(1)}, u32[]{:S(2)}, u32[]{:S(2)}) collective-permute-start(f32[2,128,256]{2,1,0:T(8,128)S(1)} %slice.7), channel_id=1, source_target_pairs={{10,1},{12,3},{14,5},{18,9},{20,11},{22,13},{26,17},{28,19},{30,21}} | collective-permute-start | bytes 786440 | tf_op jit(solution)/shard_map/ppermute | solution.py:395
  11.6 0.0 collective-permute-done.2.below_last_ref
  11.6 4.0 %collective-permute-start.5 = (f32[2,128,256]{2,1,0:T(8,128)S(1)}, f32[2,128,256]{2,1,0:T(8,128)S(1)}, u32[]{:S(2)}, u32[]{:S(2)}) collective-permute-start(f32[2,128,256]{2,1,0:T(8,128)S(1)} %collective-permute-done.2.below_last_ref), channel_id=1, source_target_pairs={{1,0},{3,2},{5,4},{7,6},{9,8},{11,10},{13,12},{15,14},{17,16},{19,... | collective-permute-start | bytes 786440 | tf_op jit(solution)/shard_map/ppermute | solution.py:400
  15.6 1.0 %collective-permute-done.1.below_first_ref = f32[2,128,256]{2,1,0:T(8,128)S(1)} collective-permute-done((f32[2,128,256]{2,1,0:T(8,128)S(1)}, f32[2,128,256]{2,1,0:T(8,128)S(1)}, u32[]{:S(2)}, u32[]{:S(2)}) %collective-permute-start.1) | collective-permute-done | bytes 262176 | tf_op jit(solution)/shard_map/ppermute | solution.py:22
  16.6 3.4 %collective-permute-start.3 = (f32[2,128,256]{2,1,0:T(8,128)S(1)}, f32[2,128,256]{2,1,0:T(8,128)S(1)}, u32[]{:S(2)}, u32[]{:S(2)}) collective-permute-start(f32[2,128,256]{2,1,0:T(8,128)S(1)} %collective-permute-done.1.below_first_ref), channel_id=1, source_target_pairs={{1,0},{2,1},{3,2},{4,3},{5,4},{6,5},{7,6},{9,8},{10,9},{11,10},{12... | collective-permute-start | bytes 786440 | tf_op jit(solution)/shard_map/ppermute | solution.py:22
  20.1 2.7 %prepare.1 = (bf16[768,256]{1,0:T(8,128)(2,1)S(1)}, bf16[256,768]{1,0:T(8,128)(2,1)S(1)}, bf16[256,768]{1,0:T(8,128)(2,1)S(1)}, bf16[768,256]{1,0:T(8,128)(2,1)S...) custom-call(f32[2,256,256]{2,1,0:T(8,128)} %measured_ref.1, ...), custom_call_target="tpu_custom_call" | custom-call | tf_op jit(solution)/shard_map/prepare/pallas_call | solution.py:297
  22.8 0.0 collective-permute-done.4.corner_last_ref
  22.8 0.0 collective-permute-done.5.relayed_ref
  22.8 2.5 %collective-permute-done.3.corner_first_ref = f32[2,128,256]{2,1,0:T(8,128)S(1)} collective-permute-done((f32[2,128,256]{2,1,0:T(8,128)S(1)}, f32[2,128,256]{2,1,0:T(8,128)S(1)}, u32[]{:S(2)}, u32[]{:S(2)}) %collective-permute-start.3) | collective-permute-done | bytes 262176 | tf_op jit(solution)/shard_map/ppermute | solution.py:22
  25.3 0.0 collective-permute-done.right_ref
  25.3 0.0 copy-done.1
  25.3 9.0 %process_scans.1 = (f32[2,256,256]{2,1,0:T(8,128)S(1)}, f32[2,256,256]{2,1,0:T(8,128)}, f32[2,256,256]{2,1,0:T(8,128)S(1)}, f32[2,256,256]{2,1,0:T(8,128)}, f32[...) custom-call(s32[2]{0:T(128)} %down_ref.1, s32[2]{0:T(128)} %across_ref.1, f32[2,256,256]{2,1,0:T(8,128)S(1)} %copy-done, ...), custom_call_target="tpu_custom_call" | custom-call | tf_op jit(solution)/shard_map/process_scans/pallas_call | solution.py:311
  34.3 0.0 collective-permute-start.10
  34.3 1.9 %collective-permute-done.10 = f32[2,256,256]{2,1,0:T(8,128)S(1)} collective-permute-done((f32[2,256,256]{2,1,0:T(8,128)S(1)}, f32[2,256,256]{2,1,0:T(8,128)S(1)}, u32[]{:S(2)}, u32[]{:S(2)}) %collective-permute-start.10) | collective-permute-done | bytes 524320 | tf_op jit(solution)/shard_map/ppermute | solution.py:26
  36.2 0.1 add.6
  36.3 12.4 %all_to_all.10.pieces_ref = f32[8,64,256]{2,1,0:T(8,128)S(1)} all-to-all(f32[8,64,256]{2,1,0:T(8,128)S(1)} %bitcast.4), channel_id=1, replica_groups={{0,2,8,10,16,18,24,26},{1,3,9,11,17,19,25,27},{4,6,12,14,20,22,28,30},{..., dimensions={0} | all-to-all | bytes 1048576 | tf_op jit(solution)/shard_map/all_to_all | solution.py:45
  48.7 1.4 %collective-permute-start.11 = (f32[64,256]{1,0:T(8,128)S(1)}, f32[64,256]{1,0:T(8,128)S(1)}, u32[]{:S(2)}, u32[]{:S(2)}) collective-permute-start(f32[64,256]{1,0:T(8,128)S(1)} %sum_pieces.1), channel_id=1, source_target_pairs={{0,4},{1,5},{2,6},{3,7},{4,0},{5,1},{6,2},{7,3},{8,12},{9,13},{10,... | collective-permute-start | bytes 196616 | tf_op jit(solution)/shard_map/ppermute | solution.py:26
  50.1 2.7 %collective-permute-done.11 = f32[64,256]{1,0:T(8,128)S(1)} collective-permute-done((f32[64,256]{1,0:T(8,128)S(1)}, f32[64,256]{1,0:T(8,128)S(1)}, u32[]{:S(2)}, u32[]{:S(2)}) %collective-permute-start.11) | collective-permute-done | bytes 65568 | tf_op jit(solution)/shard_map/ppermute | solution.py:26
  52.8 0.8 broadcast_in_dim.2
  53.7 4.5 %all-to-all-start.1 = ((f32[8,64,256]{2,1,0:T(8,128)}), f32[8,64,256]{2,1,0:T(8,128)S(1)}, u32[]{:S(2)}, u32[]{:S(2)}) async-start(f32[8,64,256]{2,1,0:T(8,128)} %broadcast_in_dim.2), calls=%async_computation.1 | async-start | bytes 1048576 | tf_op jit(solution)/shard_map/all_to_all | solution.py:50
  58.2 1.3 %collective-permute-start.7 = (f32[2,256,256]{2,1,0:T(8,128)}, f32[2,256,256]{2,1,0:T(8,128)S(1)}, u32[]{:S(2)}, u32[]{:S(2)}) collective-permute-start(f32[2,256,256]{2,1,0:T(8,128)} %get-tuple-element.29), channel_id=1, source_target_pairs={{0,1},{2,3},{4,5},{6,7},{8,9},{10,11},{12,13},{14,15},{16,17},{18,... | collective-permute-start | bytes 1572872 | tf_op jit(solution)/shard_map/ppermute | solution.py:422
  59.5 6.2 %collective-permute-start.9 = (f32[2,256,256]{2,1,0:T(8,128)}, f32[2,256,256]{2,1,0:T(8,128)S(1)}, u32[]{:S(2)}, u32[]{:S(2)}) collective-permute-start(f32[2,256,256]{2,1,0:T(8,128)} %get-tuple-element.29), channel_id=1, source_target_pairs={{1,10},{3,12},{5,14},{9,18},{11,20},{13,22},{17,26},{19,28},{21,30}} | collective-permute-start | bytes 1572872 | tf_op jit(solution)/shard_map/ppermute | solution.py:426
  65.7 1.9 %collective-permute-start.6 = (f32[2,256,256]{2,1,0:T(8,128)}, f32[2,256,256]{2,1,0:T(8,128)S(1)}, u32[]{:S(2)}, u32[]{:S(2)}) collective-permute-start(f32[2,256,256]{2,1,0:T(8,128)} %get-tuple-element.27), channel_id=1, source_target_pairs={{0,1},{1,2},{2,3},{3,4},{4,5},{5,6},{6,7},{8,9},{9,10},{10,11},{11... | collective-permute-start | bytes 1572872 | tf_op jit(solution)/shard_map/ppermute | solution.py:22
  67.6 0.0 collective-permute-done.7.refs_1_
  67.6 0.1 add_tiles.2
  67.7 1.9 %collective-permute-start.8 = (f32[2,256,256]{2,1,0:T(8,128)S(1)}, f32[2,256,256]{2,1,0:T(8,128)S(1)}, u32[]{:S(2)}, u32[]{:S(2)}) collective-permute-start(f32[2,256,256]{2,1,0:T(8,128)S(1)} %add_tiles.2), channel_id=1, source_target_pairs={{0,8},{8,16},{16,24},{1,9},{9,17},{17,25},{2,10},{10,18},{18,26},{... | collective-permute-start | bytes 1572872 | tf_op jit(solution)/shard_map/ppermute | solution.py:22
  69.6 0.0 all-to-all-done.1
  69.6 0.6 collective-permute-start.12
  70.2 7.5 %collective-permute-done.6.refs_1_ = f32[2,256,256]{2,1,0:T(8,128)S(1)} collective-permute-done((f32[2,256,256]{2,1,0:T(8,128)}, f32[2,256,256]{2,1,0:T(8,128)S(1)}, u32[]{:S(2)}, u32[]{:S(2)}) %collective-permute-start.6) | collective-permute-done | bytes 524320 | tf_op jit(solution)/shard_map/ppermute | solution.py:22
  77.7 0.0 collective-permute-done.9.refs_3_
  77.7 8.7 %collective-permute-done.8.refs_2_ = f32[2,256,256]{2,1,0:T(8,128)S(1)} collective-permute-done((f32[2,256,256]{2,1,0:T(8,128)S(1)}, f32[2,256,256]{2,1,0:T(8,128)S(1)}, u32[]{:S(2)}, u32[]{:S(2)}) %collective-permute-start.8) | collective-permute-done | bytes 524320 | tf_op jit(solution)/shard_map/ppermute | solution.py:22
  86.4 0.9 add_tiles.3
  87.3 0.8 place_mode.2.refs_0_
  88.1 0.0 collective-permute-done.12.values_ref
  88.1 0.8 place_mode.3
  (3 shorter events, 0.1 us)
Async XLA Ops:
  0.6 1.1 %copy-start = (f32[2,256,256]{2,1,0:T(8,128)S(1)}, f32[2,256,256]{2,1,0:T(8,128)}, u32[]{:S(2)}) copy-start(f32[2,256,256]{2,1,0:T(8,128)} %own_ref.1) | copy-start | bytes 1572868
  1.8 23.5 %copy-start.1 = (f32[2,2,256,256]{3,2,1,0:T(8,128)S(1)}, f32[2,2,256,256]{3,2,1,0:T(8,128)}, u32[]{:S(2)}) copy-start(f32[2,2,256,256]{3,2,1,0:T(8,128)} %probe_ref.1) | copy-start | bytes 3145732
  1.8 9.8 %collective-permute-start.2 = (f32[2,128,256]{2,1,0:T(8,128)S(1)}, f32[2,128,256]{2,1,0:T(8,128)S(1)}, u32[]{:S(2)}, u32[]{:S(2)}) collective-permute-start(f32[2,128,256]{2,1,0:T(8,128)S(1)} %slice.7), channel_id=1, source_target_pairs={{8,0},{16,8},{24,16},{9,1},{17,9},{25,17},{10,2},{18,10},{26,18},{... | collective-permute-start | bytes 786440 | tf_op jit(solution)/shard_map/ppermute | solution.py:22
  5.0 11.6 %collective-permute-start.1 = (f32[2,128,256]{2,1,0:T(8,128)S(1)}, f32[2,128,256]{2,1,0:T(8,128)S(1)}, u32[]{:S(2)}, u32[]{:S(2)}) collective-permute-start(f32[2,128,256]{2,1,0:T(8,128)S(1)} %slice.6), channel_id=1, source_target_pairs={{8,0},{16,8},{24,16},{9,1},{17,9},{25,17},{10,2},{18,10},{26,18},{... | collective-permute-start | bytes 786440 | tf_op jit(solution)/shard_map/ppermute | solution.py:22
  7.2 18.1 %collective-permute-start = (f32[2,256,256]{2,1,0:T(8,128)S(1)}, f32[2,256,256]{2,1,0:T(8,128)S(1)}, u32[]{:S(2)}, u32[]{:S(2)}) collective-permute-start(f32[2,256,256]{2,1,0:T(8,128)S(1)} %copy-done), channel_id=1, source_target_pairs={{1,0},{2,1},{3,2},{4,3},{5,4},{6,5},{7,6},{9,8},{10,9},{11,10},{12... | collective-permute-start | bytes 1572872 | tf_op jit(solution)/shard_map/ppermute | solution.py:22
  10.3 12.5 %collective-permute-start.4 = (f32[2,128,256]{2,1,0:T(8,128)S(1)}, f32[2,128,256]{2,1,0:T(8,128)S(1)}, u32[]{:S(2)}, u32[]{:S(2)}) collective-permute-start(f32[2,128,256]{2,1,0:T(8,128)S(1)} %slice.7), channel_id=1, source_target_pairs={{10,1},{12,3},{14,5},{18,9},{20,11},{22,13},{26,17},{28,19},{30,21}} | collective-permute-start | bytes 786440 | tf_op jit(solution)/shard_map/ppermute | solution.py:395
  11.6 11.2 %collective-permute-start.5 = (f32[2,128,256]{2,1,0:T(8,128)S(1)}, f32[2,128,256]{2,1,0:T(8,128)S(1)}, u32[]{:S(2)}, u32[]{:S(2)}) collective-permute-start(f32[2,128,256]{2,1,0:T(8,128)S(1)} %collective-permute-done.2.below_last_ref), channel_id=1, source_target_pairs={{1,0},{3,2},{5,4},{7,6},{9,8},{11,10},{13,12},{15,14},{17,16},{19,... | collective-permute-start | bytes 786440 | tf_op jit(solution)/shard_map/ppermute | solution.py:400
  16.6 8.7 %collective-permute-start.3 = (f32[2,128,256]{2,1,0:T(8,128)S(1)}, f32[2,128,256]{2,1,0:T(8,128)S(1)}, u32[]{:S(2)}, u32[]{:S(2)}) collective-permute-start(f32[2,128,256]{2,1,0:T(8,128)S(1)} %collective-permute-done.1.below_first_ref), channel_id=1, source_target_pairs={{1,0},{2,1},{3,2},{4,3},{5,4},{6,5},{7,6},{9,8},{10,9},{11,10},{12... | collective-permute-start | bytes 786440 | tf_op jit(solution)/shard_map/ppermute | solution.py:22
  34.3 1.9 %collective-permute-start.10 = (f32[2,256,256]{2,1,0:T(8,128)S(1)}, f32[2,256,256]{2,1,0:T(8,128)S(1)}, u32[]{:S(2)}, u32[]{:S(2)}) collective-permute-start(f32[2,256,256]{2,1,0:T(8,128)S(1)} %get-tuple-element.31), channel_id=1, source_target_pairs={{0,1},{1,0},{2,3},{3,2},{4,5},{5,4},{6,7},{7,6},{8,9},{9,8},{10,11... | collective-permute-start | bytes 1572872 | tf_op jit(solution)/shard_map/ppermute | solution.py:26
  48.7 4.1 %collective-permute-start.11 = (f32[64,256]{1,0:T(8,128)S(1)}, f32[64,256]{1,0:T(8,128)S(1)}, u32[]{:S(2)}, u32[]{:S(2)}) collective-permute-start(f32[64,256]{1,0:T(8,128)S(1)} %sum_pieces.1), channel_id=1, source_target_pairs={{0,4},{1,5},{2,6},{3,7},{4,0},{5,1},{6,2},{7,3},{8,12},{9,13},{10,... | collective-permute-start | bytes 196616 | tf_op jit(solution)/shard_map/ppermute | solution.py:26
  53.7 16.0 %all-to-all-start.1 = ((f32[8,64,256]{2,1,0:T(8,128)}), f32[8,64,256]{2,1,0:T(8,128)S(1)}, u32[]{:S(2)}, u32[]{:S(2)}) async-start(f32[8,64,256]{2,1,0:T(8,128)} %broadcast_in_dim.2), calls=%async_computation.1 | async-start | bytes 1048576 | tf_op jit(solution)/shard_map/all_to_all | solution.py:50
  58.2 9.4 %collective-permute-start.7 = (f32[2,256,256]{2,1,0:T(8,128)}, f32[2,256,256]{2,1,0:T(8,128)S(1)}, u32[]{:S(2)}, u32[]{:S(2)}) collective-permute-start(f32[2,256,256]{2,1,0:T(8,128)} %get-tuple-element.29), channel_id=1, source_target_pairs={{0,1},{2,3},{4,5},{6,7},{8,9},{10,11},{12,13},{14,15},{16,17},{18,... | collective-permute-start | bytes 1572872 | tf_op jit(solution)/shard_map/ppermute | solution.py:422
  59.5 18.3 %collective-permute-start.9 = (f32[2,256,256]{2,1,0:T(8,128)}, f32[2,256,256]{2,1,0:T(8,128)S(1)}, u32[]{:S(2)}, u32[]{:S(2)}) collective-permute-start(f32[2,256,256]{2,1,0:T(8,128)} %get-tuple-element.29), channel_id=1, source_target_pairs={{1,10},{3,12},{5,14},{9,18},{11,20},{13,22},{17,26},{19,28},{21,30}} | collective-permute-start | bytes 1572872 | tf_op jit(solution)/shard_map/ppermute | solution.py:426
  65.7 12.1 %collective-permute-start.6 = (f32[2,256,256]{2,1,0:T(8,128)}, f32[2,256,256]{2,1,0:T(8,128)S(1)}, u32[]{:S(2)}, u32[]{:S(2)}) collective-permute-start(f32[2,256,256]{2,1,0:T(8,128)} %get-tuple-element.27), channel_id=1, source_target_pairs={{0,1},{1,2},{2,3},{3,4},{4,5},{5,6},{6,7},{8,9},{9,10},{10,11},{11... | collective-permute-start | bytes 1572872 | tf_op jit(solution)/shard_map/ppermute | solution.py:22
  67.7 18.8 %collective-permute-start.8 = (f32[2,256,256]{2,1,0:T(8,128)S(1)}, f32[2,256,256]{2,1,0:T(8,128)S(1)}, u32[]{:S(2)}, u32[]{:S(2)}) collective-permute-start(f32[2,256,256]{2,1,0:T(8,128)S(1)} %add_tiles.2), channel_id=1, source_target_pairs={{0,8},{8,16},{16,24},{1,9},{9,17},{17,25},{2,10},{10,18},{18,26},{... | collective-permute-start | bytes 1572872 | tf_op jit(solution)/shard_map/ppermute | solution.py:22
  69.6 18.5 %collective-permute-start.12 = (f32[2,256,256]{2,1,0:T(8,128)S(1)}, f32[2,256,256]{2,1,0:T(8,128)S(1)}, u32[]{:S(2)}, u32[]{:S(2)}) collective-permute-start(f32[2,256,256]{2,1,0:T(8,128)S(1)} %bitcast.2), channel_id=1, source_target_pairs={{0,1},{1,0},{2,3},{3,2},{4,5},{5,4},{6,7},{7,6},{8,9},{9,8},{10,11... | collective-permute-start | bytes 1572872 | tf_op jit(solution)/shard_map/ppermute | solution.py:26

commit v4 on v3

--- a/solution.py
+++ b/solution.py
@@ -136,7 +136,6 @@
     below_last_ref,
     corner_first_ref,
     corner_last_ref,
-    relayed_ref,
     probe_ref,
     measured_ref,
     right_f_ref,
@@ -181,8 +180,7 @@
         patch = []
         for part in range(2):
             below = jnp.concatenate([below_first_ref[part], below_last_ref[part]], axis=0)
-            corner_last = corner_last_ref[part] + relayed_ref[part]
-            corner = jnp.concatenate([corner_first_ref[part], corner_last], axis=0)
+            corner = jnp.concatenate([corner_first_ref[part], corner_last_ref[part]], axis=0)
             merged = jnp.where(
                 later_row,
                 jnp.where(later_col, corner, below),
@@ -381,28 +379,27 @@
     core = lax.rem(lax.axis_index("col"), 2)
     table = tables(length)
 
-    middle = transmission.shape[1] // 2
+    middle = transmission.shape[1] * 9 // 16 // 8 * 8
     first, rest = lax.optimization_barrier((transmission[:, :middle], transmission))
     last = rest[:, middle:]
-    direct = [
+    diagonal = [
         ((row + 1) * cols + col + 1, row * cols + col)
         for row in range(rows - 1)
-        for col in range(1, cols - 1, 2)
+        for col in range(cols - 1)
     ]
+    direct = [(start, end) for start, end in diagonal if end % cols % 2 == 1]
     below_first = shifted(first, "row", -1)
     below_last = shifted(last, "row", -1)
     right = shifted(transmission, "col", -1)
-    corner_last = lax.ppermute(last, ("row", "col"), direct)
+    corner_last = lax.ppermute(last, ("row", "col"), diagonal)
     corner_first = shifted(below_first, "col", -1)
     consts = [table[name] for name in ("right_f", "left_f", "left_b", "right_b", "lane", "sub")]
     picks = [table["pick_rows"], table["pick_cols"]]
     *consts, ordered = prepare(measured, picks, consts)
-    relayed = lax.ppermute(below_last, "col", [(col + 1, col) for col in range(0, cols - 1, 2)])
-
     offsets = (offset_down, offset_across)
     own, to_right, to_below, to_corner, keep, send = process_scans(
         offsets,
-        (transmission, right, below_first, below_last, corner_first, corner_last, relayed),
+        (transmission, right, below_first, below_last, corner_first, corner_last),
         probe_modes,
         ordered,
         consts,

time: 89.5 us -> 94.2 us (1.053)
  waiting for transfers between devices: 24.4 us -> 30 us
  starting transfers between devices: 34.9 us -> 33.5 us
    ppermute x6, waiting for transfers between devices: 19.8 us -> 24.3 us  [shifted(): return lax.ppermute(block, axis, route)]
    ppermute x2 -> x1, waiting for transfers between devices: 0.01 us -> 1.43 us  [on_device(): corner_last = lax.ppermute(last, ('row', 'col'), diagonal)]
    ppermute x2 -> x1, starting transfers between devices: 5.24 us -> 3.99 us  [on_device(): corner_last = lax.ppermute(last, ('row', 'col'), diagonal)]
  transfers between devices with their start and end apart: 14 -> 13, of which waited for: 6 -> 7; matrix products, arithmetic and copies ran while one was open for 0% -> 0% of each run, Pallas kernels for 5% -> 5%
where the time goes in v4:
time: 94.2 us; the launch traced here: 93.7 us
  starting transfers between devices  33.5 us (36%)
  waiting for transfers between devices  30 us (32%)
  Pallas kernels  14.3 us (15%)
  blocking collectives  13.1 us (14%)
  local copies, waits for them, and re-layouts  1.91 us (2%)
    ppermute x6, waiting for transfers between devices, shifted(): return lax.ppermute(block, axis, route)  24.3 us
    ppermute x6, starting transfers between devices, shifted(): return lax.ppermute(block, axis, route)  15.2 us
    all_to_all x1, blocking collectives, scatter_sum(): lax.all_to_all(pieces, ('row', 'col'), 0, 0, axis_index_groups=groups)  13.1 us
    pallas_call x1, Pallas kernels, process_scans(): pl.pallas_call(scan_kernel, out_shape=[VMEM(shape, jnp.float32) for shape...  9.01 us
    ppermute x1, starting transfers between devices, on_device(): lax.ppermute(to_corner, ('row', 'col'), [(end, start) for start, end in d...  6.23 us
    all_to_all x1, starting transfers between devices, gather_slices(): lax.all_to_all(copies, ('row', 'col'), 0, 0, axis_index_groups=groups)  4.51 us
    ppermute x3, waiting for transfers between devices, swapped(): lax.ppermute(block, axis, [(i, i ^ mask) for i in range(lax.axis_size(axi...  4.26 us
    ppermute x1, starting transfers between devices, on_device(): corner_last = lax.ppermute(last, ('row', 'col'), diagonal)  3.99 us
  transfers between devices with their start and end apart: 13, of which 7 were waited for; matrix products, arithmetic and copies ran while one was open for 0% of the time, Pallas kernels for 5%

profile of v4, /device:TPU:13, one launch (start us, length us, event | category | flops | bytes accessed | tf_op | source)
XLA Modules:
  0.0 93.7 jit_solution(1584055246914677803)
XLA Ops:
  0.6 0.0 copy-start
  0.6 1.0 %slice.6 = f32[2,144,256]{2,1,0:T(8,128)S(1)} slice(f32[2,256,256]{2,1,0:T(8,128)} %own_ref.1), slice={[0:2], [0:144], [0:256]} | slice | bytes 589824 | tf_op jit(solution)/shard_map/slice | solution.py:383
  1.7 3.1 %collective-permute-start.1 = (f32[2,144,256]{2,1,0:T(8,128)S(1)}, f32[2,144,256]{2,1,0:T(8,128)S(1)}, u32[]{:S(2)}, u32[]{:S(2)}) collective-permute-start(f32[2,144,256]{2,1,0:T(8,128)S(1)} %slice.6), channel_id=1, source_target_pairs={{8,0},{16,8},{24,16},{9,1},{17,9},{25,17},{10,2},{18,10},{26,18},{... | collective-permute-start | bytes 884744 | tf_op jit(solution)/shard_map/ppermute | solution.py:22
  4.8 0.0 copy-done
  4.8 2.9 %collective-permute-start = (f32[2,256,256]{2,1,0:T(8,128)S(1)}, f32[2,256,256]{2,1,0:T(8,128)S(1)}, u32[]{:S(2)}, u32[]{:S(2)}) collective-permute-start(f32[2,256,256]{2,1,0:T(8,128)S(1)} %copy-done), channel_id=1, source_target_pairs={{1,0},{2,1},{3,2},{4,3},{5,4},{6,5},{7,6},{9,8},{10,9},{11,10},{12... | collective-permute-start | bytes 1572872 | tf_op jit(solution)/shard_map/ppermute | solution.py:22
  7.6 3.8 %collective-permute-done.1.below_first_ref = f32[2,144,256]{2,1,0:T(8,128)S(1)} collective-permute-done((f32[2,144,256]{2,1,0:T(8,128)S(1)}, f32[2,144,256]{2,1,0:T(8,128)S(1)}, u32[]{:S(2)}, u32[]{:S(2)}) %collective-permute-start.1) | collective-permute-done | bytes 294944 | tf_op jit(solution)/shard_map/ppermute | solution.py:22
  11.5 3.4 %collective-permute-start.3 = (f32[2,144,256]{2,1,0:T(8,128)S(1)}, f32[2,144,256]{2,1,0:T(8,128)S(1)}, u32[]{:S(2)}, u32[]{:S(2)}) collective-permute-start(f32[2,144,256]{2,1,0:T(8,128)S(1)} %collective-permute-done.1.below_first_ref), channel_id=1, source_target_pairs={{1,0},{2,1},{3,2},{4,3},{5,4},{6,5},{7,6},{9,8},{10,9},{11,10},{12... | collective-permute-start | bytes 884744 | tf_op jit(solution)/shard_map/ppermute | solution.py:22
  14.9 0.0 copy-start.1
  14.9 4.0 %collective-permute-start.4 = (f32[2,112,256]{2,1,0:T(8,128)S(1)}, f32[2,112,256]{2,1,0:T(8,128)S(1)}, u32[]{:S(2)}, u32[]{:S(2)}) collective-permute-start(f32[2,112,256]{2,1,0:T(8,128)S(1)} %slice.7), channel_id=1, source_target_pairs={{9,0},{10,1},{11,2},{12,3},{13,4},{14,5},{15,6},{17,8},{18,9},{19,... | collective-permute-start | bytes 688136 | tf_op jit(solution)/shard_map/ppermute | solution.py:394
  18.9 2.0 %collective-permute-start.2 = (f32[2,112,256]{2,1,0:T(8,128)S(1)}, f32[2,112,256]{2,1,0:T(8,128)S(1)}, u32[]{:S(2)}, u32[]{:S(2)}) collective-permute-start(f32[2,112,256]{2,1,0:T(8,128)S(1)} %slice.7), channel_id=1, source_target_pairs={{8,0},{16,8},{24,16},{9,1},{17,9},{25,17},{10,2},{18,10},{26,18},{... | collective-permute-start | bytes 688136 | tf_op jit(solution)/shard_map/ppermute | solution.py:22
  21.0 2.7 %prepare.1 = (bf16[768,256]{1,0:T(8,128)(2,1)S(1)}, bf16[256,768]{1,0:T(8,128)(2,1)S(1)}, bf16[256,768]{1,0:T(8,128)(2,1)S(1)}, bf16[768,256]{1,0:T(8,128)(2,1)S...) custom-call(f32[2,256,256]{2,1,0:T(8,128)} %measured_ref.1, ...), custom_call_target="tpu_custom_call" | custom-call | tf_op jit(solution)/shard_map/prepare/pallas_call | solution.py:295
  23.7 1.4 %collective-permute-done.4.corner_last_ref = f32[2,112,256]{2,1,0:T(8,128)S(1)} collective-permute-done((f32[2,112,256]{2,1,0:T(8,128)S(1)}, f32[2,112,256]{2,1,0:T(8,128)S(1)}, u32[]{:S(2)}, u32[]{:S(2)}) %collective-permute-start.4) | collective-permute-done | bytes 229408 | tf_op jit(solution)/shard_map/ppermute | solution.py:394
  25.1 4.2 %collective-permute-done.2.below_last_ref = f32[2,112,256]{2,1,0:T(8,128)S(1)} collective-permute-done((f32[2,112,256]{2,1,0:T(8,128)S(1)}, f32[2,112,256]{2,1,0:T(8,128)S(1)}, u32[]{:S(2)}, u32[]{:S(2)}) %collective-permute-start.2) | collective-permute-done | bytes 229408 | tf_op jit(solution)/shard_map/ppermute | solution.py:22
  29.3 0.0 collective-permute-done.right_ref
  29.3 0.0 collective-permute-done.3.corner_first_ref
  29.3 0.0 copy-done.1
  29.3 9.0 %process_scans.1 = (f32[2,256,256]{2,1,0:T(8,128)S(1)}, f32[2,256,256]{2,1,0:T(8,128)}, f32[2,256,256]{2,1,0:T(8,128)S(1)}, f32[2,256,256]{2,1,0:T(8,128)}, f32[...) custom-call(s32[2]{0:T(128)} %down_ref.1, s32[2]{0:T(128)} %across_ref.1, f32[2,256,256]{2,1,0:T(8,128)S(1)} %copy-done, ...), custom_call_target="tpu_custom_call" | custom-call | tf_op jit(solution)/shard_map/process_scans/pallas_call | solution.py:309
  38.3 0.4 collective-permute-start.9
  38.7 1.5 %collective-permute-done.9 = f32[2,256,256]{2,1,0:T(8,128)S(1)} collective-permute-done((f32[2,256,256]{2,1,0:T(8,128)S(1)}, f32[2,256,256]{2,1,0:T(8,128)S(1)}, u32[]{:S(2)}, u32[]{:S(2)}) %collective-permute-start.9) | collective-permute-done | bytes 524320 | tf_op jit(solution)/shard_map/ppermute | solution.py:26
  40.3 0.1 add.6
  40.3 13.1 %all_to_all.10.pieces_ref = f32[8,64,256]{2,1,0:T(8,128)S(1)} all-to-all(f32[8,64,256]{2,1,0:T(8,128)S(1)} %bitcast.4), channel_id=1, replica_groups={{0,2,8,10,16,18,24,26},{1,3,9,11,17,19,25,27},{4,6,12,14,20,22,28,30},{..., dimensions={0} | all-to-all | bytes 1048576 | tf_op jit(solution)/shard_map/all_to_all | solution.py:45
  53.4 1.4 %collective-permute-start.10 = (f32[64,256]{1,0:T(8,128)S(1)}, f32[64,256]{1,0:T(8,128)S(1)}, u32[]{:S(2)}, u32[]{:S(2)}) collective-permute-start(f32[64,256]{1,0:T(8,128)S(1)} %sum_pieces.1), channel_id=1, source_target_pairs={{0,4},{1,5},{2,6},{3,7},{4,0},{5,1},{6,2},{7,3},{8,12},{9,13},{10,... | collective-permute-start | bytes 196616 | tf_op jit(solution)/shard_map/ppermute | solution.py:26
  54.8 2.7 %collective-permute-done.10 = f32[64,256]{1,0:T(8,128)S(1)} collective-permute-done((f32[64,256]{1,0:T(8,128)S(1)}, f32[64,256]{1,0:T(8,128)S(1)}, u32[]{:S(2)}, u32[]{:S(2)}) %collective-permute-start.10) | collective-permute-done | bytes 65568 | tf_op jit(solution)/shard_map/ppermute | solution.py:26
  57.5 0.8 broadcast_in_dim.2
  58.4 4.5 %all-to-all-start.1 = ((f32[8,64,256]{2,1,0:T(8,128)}), f32[8,64,256]{2,1,0:T(8,128)S(1)}, u32[]{:S(2)}, u32[]{:S(2)}) async-start(f32[8,64,256]{2,1,0:T(8,128)} %broadcast_in_dim.2), calls=%async_computation.1 | async-start | bytes 1048576 | tf_op jit(solution)/shard_map/all_to_all | solution.py:50
  62.9 1.3 %collective-permute-start.6 = (f32[2,256,256]{2,1,0:T(8,128)}, f32[2,256,256]{2,1,0:T(8,128)S(1)}, u32[]{:S(2)}, u32[]{:S(2)}) collective-permute-start(f32[2,256,256]{2,1,0:T(8,128)} %get-tuple-element.29), channel_id=1, source_target_pairs={{0,1},{2,3},{4,5},{6,7},{8,9},{10,11},{12,13},{14,15},{16,17},{18,... | collective-permute-start | bytes 1572872 | tf_op jit(solution)/shard_map/ppermute | solution.py:419
  64.2 6.2 %collective-permute-start.8 = (f32[2,256,256]{2,1,0:T(8,128)}, f32[2,256,256]{2,1,0:T(8,128)S(1)}, u32[]{:S(2)}, u32[]{:S(2)}) collective-permute-start(f32[2,256,256]{2,1,0:T(8,128)} %get-tuple-element.29), channel_id=1, source_target_pairs={{1,10},{3,12},{5,14},{9,18},{11,20},{13,22},{17,26},{19,28},{21,30}} | collective-permute-start | bytes 1572872 | tf_op jit(solution)/shard_map/ppermute | solution.py:423
  70.4 1.9 %collective-permute-start.5 = (f32[2,256,256]{2,1,0:T(8,128)}, f32[2,256,256]{2,1,0:T(8,128)S(1)}, u32[]{:S(2)}, u32[]{:S(2)}) collective-permute-start(f32[2,256,256]{2,1,0:T(8,128)} %get-tuple-element.27), channel_id=1, source_target_pairs={{0,1},{1,2},{2,3},{3,4},{4,5},{5,6},{6,7},{8,9},{9,10},{10,11},{11... | collective-permute-start | bytes 1572872 | tf_op jit(solution)/shard_map/ppermute | solution.py:22
  72.3 0.0 collective-permute-done.6.refs_1_
  72.3 0.1 add_tiles.2
  72.4 1.9 %collective-permute-start.7 = (f32[2,256,256]{2,1,0:T(8,128)S(1)}, f32[2,256,256]{2,1,0:T(8,128)S(1)}, u32[]{:S(2)}, u32[]{:S(2)}) collective-permute-start(f32[2,256,256]{2,1,0:T(8,128)S(1)} %add_tiles.2), channel_id=1, source_target_pairs={{0,8},{8,16},{16,24},{1,9},{9,17},{17,25},{2,10},{10,18},{18,26},{... | collective-permute-start | bytes 1572872 | tf_op jit(solution)/shard_map/ppermute | solution.py:22
  74.3 0.0 all-to-all-done.1
  74.3 0.6 collective-permute-start.11
  74.9 7.5 %collective-permute-done.5.refs_1_ = f32[2,256,256]{2,1,0:T(8,128)S(1)} collective-permute-done((f32[2,256,256]{2,1,0:T(8,128)}, f32[2,256,256]{2,1,0:T(8,128)S(1)}, u32[]{:S(2)}, u32[]{:S(2)}) %collective-permute-start.5) | collective-permute-done | bytes 524320 | tf_op jit(solution)/shard_map/ppermute | solution.py:22
  82.4 0.0 collective-permute-done.8.refs_3_
  82.4 8.7 %collective-permute-done.7.refs_2_ = f32[2,256,256]{2,1,0:T(8,128)S(1)} collective-permute-done((f32[2,256,256]{2,1,0:T(8,128)S(1)}, f32[2,256,256]{2,1,0:T(8,128)S(1)}, u32[]{:S(2)}, u32[]{:S(2)}) %collective-permute-start.7) | collective-permute-done | bytes 524320 | tf_op jit(solution)/shard_map/ppermute | solution.py:22
  91.1 0.9 add_tiles.3
  92.0 0.8 place_mode.2.refs_0_
  92.8 0.0 collective-permute-done.11.values_ref
  92.8 0.8 place_mode.3
  (3 shorter events, 0.1 us)
Async XLA Ops:
  0.6 4.1 %copy-start = (f32[2,256,256]{2,1,0:T(8,128)S(1)}, f32[2,256,256]{2,1,0:T(8,128)}, u32[]{:S(2)}) copy-start(f32[2,256,256]{2,1,0:T(8,128)} %own_ref.1) | copy-start | bytes 1572868
  1.7 9.8 %collective-permute-start.1 = (f32[2,144,256]{2,1,0:T(8,128)S(1)}, f32[2,144,256]{2,1,0:T(8,128)S(1)}, u32[]{:S(2)}, u32[]{:S(2)}) collective-permute-start(f32[2,144,256]{2,1,0:T(8,128)S(1)} %slice.6), channel_id=1, source_target_pairs={{8,0},{16,8},{24,16},{9,1},{17,9},{25,17},{10,2},{18,10},{26,18},{... | collective-permute-start | bytes 884744 | tf_op jit(solution)/shard_map/ppermute | solution.py:22
  4.8 24.5 %collective-permute-start = (f32[2,256,256]{2,1,0:T(8,128)S(1)}, f32[2,256,256]{2,1,0:T(8,128)S(1)}, u32[]{:S(2)}, u32[]{:S(2)}) collective-permute-start(f32[2,256,256]{2,1,0:T(8,128)S(1)} %copy-done), channel_id=1, source_target_pairs={{1,0},{2,1},{3,2},{4,3},{5,4},{6,5},{7,6},{9,8},{10,9},{11,10},{12... | collective-permute-start | bytes 1572872 | tf_op jit(solution)/shard_map/ppermute | solution.py:22
  11.5 17.8 %collective-permute-start.3 = (f32[2,144,256]{2,1,0:T(8,128)S(1)}, f32[2,144,256]{2,1,0:T(8,128)S(1)}, u32[]{:S(2)}, u32[]{:S(2)}) collective-permute-start(f32[2,144,256]{2,1,0:T(8,128)S(1)} %collective-permute-done.1.below_first_ref), channel_id=1, source_target_pairs={{1,0},{2,1},{3,2},{4,3},{5,4},{6,5},{7,6},{9,8},{10,9},{11,10},{12... | collective-permute-start | bytes 884744 | tf_op jit(solution)/shard_map/ppermute | solution.py:22
  14.9 14.4 %copy-start.1 = (f32[2,2,256,256]{3,2,1,0:T(8,128)S(1)}, f32[2,2,256,256]{3,2,1,0:T(8,128)}, u32[]{:S(2)}) copy-start(f32[2,2,256,256]{3,2,1,0:T(8,128)} %probe_ref.1) | copy-start | bytes 3145732
  14.9 10.2 %collective-permute-start.4 = (f32[2,112,256]{2,1,0:T(8,128)S(1)}, f32[2,112,256]{2,1,0:T(8,128)S(1)}, u32[]{:S(2)}, u32[]{:S(2)}) collective-permute-start(f32[2,112,256]{2,1,0:T(8,128)S(1)} %slice.7), channel_id=1, source_target_pairs={{9,0},{10,1},{11,2},{12,3},{13,4},{14,5},{15,6},{17,8},{18,9},{19,... | collective-permute-start | bytes 688136 | tf_op jit(solution)/shard_map/ppermute | solution.py:394
  18.9 10.4 %collective-permute-start.2 = (f32[2,112,256]{2,1,0:T(8,128)S(1)}, f32[2,112,256]{2,1,0:T(8,128)S(1)}, u32[]{:S(2)}, u32[]{:S(2)}) collective-permute-start(f32[2,112,256]{2,1,0:T(8,128)S(1)} %slice.7), channel_id=1, source_target_pairs={{8,0},{16,8},{24,16},{9,1},{17,9},{25,17},{10,2},{18,10},{26,18},{... | collective-permute-start | bytes 688136 | tf_op jit(solution)/shard_map/ppermute | solution.py:22
  38.3 1.9 %collective-permute-start.9 = (f32[2,256,256]{2,1,0:T(8,128)S(1)}, f32[2,256,256]{2,1,0:T(8,128)S(1)}, u32[]{:S(2)}, u32[]{:S(2)}) collective-permute-start(f32[2,256,256]{2,1,0:T(8,128)S(1)} %get-tuple-element.31), channel_id=1, source_target_pairs={{0,1},{1,0},{2,3},{3,2},{4,5},{5,4},{6,7},{7,6},{8,9},{9,8},{10,11... | collective-permute-start | bytes 1572872 | tf_op jit(solution)/shard_map/ppermute | solution.py:26
  53.4 4.1 %collective-permute-start.10 = (f32[64,256]{1,0:T(8,128)S(1)}, f32[64,256]{1,0:T(8,128)S(1)}, u32[]{:S(2)}, u32[]{:S(2)}) collective-permute-start(f32[64,256]{1,0:T(8,128)S(1)} %sum_pieces.1), channel_id=1, source_target_pairs={{0,4},{1,5},{2,6},{3,7},{4,0},{5,1},{6,2},{7,3},{8,12},{9,13},{10,... | collective-permute-start | bytes 196616 | tf_op jit(solution)/shard_map/ppermute | solution.py:26
  58.4 16.0 %all-to-all-start.1 = ((f32[8,64,256]{2,1,0:T(8,128)}), f32[8,64,256]{2,1,0:T(8,128)S(1)}, u32[]{:S(2)}, u32[]{:S(2)}) async-start(f32[8,64,256]{2,1,0:T(8,128)} %broadcast_in_dim.2), calls=%async_computation.1 | async-start | bytes 1048576 | tf_op jit(solution)/shard_map/all_to_all | solution.py:50
  62.9 9.5 %collective-permute-start.6 = (f32[2,256,256]{2,1,0:T(8,128)}, f32[2,256,256]{2,1,0:T(8,128)S(1)}, u32[]{:S(2)}, u32[]{:S(2)}) collective-permute-start(f32[2,256,256]{2,1,0:T(8,128)} %get-tuple-element.29), channel_id=1, source_target_pairs={{0,1},{2,3},{4,5},{6,7},{8,9},{10,11},{12,13},{14,15},{16,17},{18,... | collective-permute-start | bytes 1572872 | tf_op jit(solution)/shard_map/ppermute | solution.py:419
  64.2 18.3 %collective-permute-start.8 = (f32[2,256,256]{2,1,0:T(8,128)}, f32[2,256,256]{2,1,0:T(8,128)S(1)}, u32[]{:S(2)}, u32[]{:S(2)}) collective-permute-start(f32[2,256,256]{2,1,0:T(8,128)} %get-tuple-element.29), channel_id=1, source_target_pairs={{1,10},{3,12},{5,14},{9,18},{11,20},{13,22},{17,26},{19,28},{21,30}} | collective-permute-start | bytes 1572872 | tf_op jit(solution)/shard_map/ppermute | solution.py:423
  70.4 12.1 %collective-permute-start.5 = (f32[2,256,256]{2,1,0:T(8,128)}, f32[2,256,256]{2,1,0:T(8,128)S(1)}, u32[]{:S(2)}, u32[]{:S(2)}) collective-permute-start(f32[2,256,256]{2,1,0:T(8,128)} %get-tuple-element.27), channel_id=1, source_target_pairs={{0,1},{1,2},{2,3},{3,4},{4,5},{5,6},{6,7},{8,9},{9,10},{10,11},{11... | collective-permute-start | bytes 1572872 | tf_op jit(solution)/shard_map/ppermute | solution.py:22
  72.4 18.7 %collective-permute-start.7 = (f32[2,256,256]{2,1,0:T(8,128)S(1)}, f32[2,256,256]{2,1,0:T(8,128)S(1)}, u32[]{:S(2)}, u32[]{:S(2)}) collective-permute-start(f32[2,256,256]{2,1,0:T(8,128)S(1)} %add_tiles.2), channel_id=1, source_target_pairs={{0,8},{8,16},{16,24},{1,9},{9,17},{17,25},{2,10},{10,18},{18,26},{... | collective-permute-start | bytes 1572872 | tf_op jit(solution)/shard_map/ppermute | solution.py:22
  74.3 18.5 %collective-permute-start.11 = (f32[2,256,256]{2,1,0:T(8,128)S(1)}, f32[2,256,256]{2,1,0:T(8,128)S(1)}, u32[]{:S(2)}, u32[]{:S(2)}) collective-permute-start(f32[2,256,256]{2,1,0:T(8,128)S(1)} %bitcast.2), channel_id=1, source_target_pairs={{0,1},{1,0},{2,3},{3,2},{4,5},{5,4},{6,7},{7,6},{8,9},{9,8},{10,11... | collective-permute-start | bytes 1572872 | tf_op jit(solution)/shard_map/ppermute | solution.py:26

commit v5 on v4

--- a/solution.py
+++ b/solution.py
@@ -148,6 +148,7 @@
     right_out,
     below_out,
     corner_out,
+    again_out,
     keep_out,
     send_out,
     wave_ref,
@@ -279,6 +280,8 @@
                     out[part] = piece
                 else:
                     out[part] = out[part] + piece
+        if which == scans - 1:
+            again_out[...] = corner_out[...]
 
 
 def in_space(space, *arrays):
@@ -305,7 +308,7 @@
 def process_scans(offsets, tiles, probe_modes, measured, consts):
     modes, _, length, _ = probe_modes.shape
     operands = in_space(VMEM, *tiles, probe_modes, measured, *consts)
-    results = [tiles[0].shape] * 4 + [probe_modes.shape[1:]] * 2
+    results = [tiles[0].shape] * 5 + [probe_modes.shape[1:]] * 2
     return pl.pallas_call(
         scan_kernel,
         out_shape=[VMEM(shape, jnp.float32) for shape in results],
@@ -397,7 +400,7 @@
     picks = [table["pick_rows"], table["pick_cols"]]
     *consts, ordered = prepare(measured, picks, consts)
     offsets = (offset_down, offset_across)
-    own, to_right, to_below, to_corner, keep, send = process_scans(
+    own, to_right, to_below, to_corner, to_corner_again, keep, send = process_scans(
         offsets,
         (transmission, right, below_first, below_last, corner_first, corner_last),
         probe_modes,
@@ -420,7 +423,7 @@
     to_below = add_tiles(to_below, relayed, out=VMEM(to_below.shape, jnp.float32))
     from_left = shifted(to_right, "col", 1)
     from_above = shifted(to_below, "row", 1)
-    from_corner = lax.ppermute(to_corner, ("row", "col"), [(end, start) for start, end in direct])
+    from_corner = lax.ppermute(to_corner_again, ("row", "col"), [(end, start) for start, end in direct])
     tile = jax.ShapeDtypeStruct(own.shape, jnp.float32)
     own = add_tiles(own, from_left, from_above, from_corner, out=tile)
     return own, probe_gradient

time: 94.2 us -> 96.7 us (1.027)
  waiting for transfers between devices: 30 us -> 32.8 us
    ppermute x1, waiting for transfers between devices: 0.01 us -> 5.67 us  [on_device(): lax.ppermute(to_corner_again, ('row', 'col'), [(end, start) for start, en...]
    ppermute x6, starting transfers between devices: 15.2 us -> 18.6 us  [shifted(): return lax.ppermute(block, axis, route)]
    ppermute x1, starting transfers between devices: 6.23 us -> 2.86 us  [on_device(): lax.ppermute(to_corner_again, ('row', 'col'), [(end, start) for start, en...]
    ppermute x6, waiting for transfers between devices: 24.3 us -> 21.4 us  [shifted(): return lax.ppermute(block, axis, route)]
  transfers between devices with their start and end apart: 13 -> 13, of which waited for: 7 -> 8; matrix products, arithmetic and copies ran while one was open for 0% -> 0% of each run, Pallas kernels for 5% -> 5%
where the time goes in v5:
time: 96.7 us; the launch traced here: 96.2 us
  starting transfers between devices  33.3 us (34%)
  waiting for transfers between devices  32.8 us (34%)
  Pallas kernels  14.3 us (15%)
  blocking collectives  13.1 us (14%)
  local copies, waits for them, and re-layouts  1.91 us (2%)
    ppermute x6, waiting for transfers between devices, shifted(): return lax.ppermute(block, axis, route)  21.4 us
    ppermute x6, starting transfers between devices, shifted(): return lax.ppermute(block, axis, route)  18.6 us
    all_to_all x1, blocking collectives, scatter_sum(): lax.all_to_all(pieces, ('row', 'col'), 0, 0, axis_index_groups=groups)  13.1 us
    pallas_call x1, Pallas kernels, process_scans(): pl.pallas_call(scan_kernel, out_shape=[VMEM(shape, jnp.float32) for shape...  9.02 us
    ppermute x1, waiting for transfers between devices, on_device(): lax.ppermute(to_corner_again, ('row', 'col'), [(end, start) for start, en...  5.67 us
    all_to_all x1, starting transfers between devices, gather_slices(): lax.all_to_all(copies, ('row', 'col'), 0, 0, axis_index_groups=groups)  4.51 us
    ppermute x3, waiting for transfers between devices, swapped(): lax.ppermute(block, axis, [(i, i ^ mask) for i in range(lax.axis_size(axi...  4.26 us
    ppermute x1, starting transfers between devices, on_device(): corner_last = lax.ppermute(last, ('row', 'col'), diagonal)  3.99 us
  transfers between devices with their start and end apart: 13, of which 8 were waited for; matrix products, arithmetic and copies ran while one was open for 0% of the time, Pallas kernels for 5%

profile of v5, /device:TPU:13, one launch (start us, length us, event | category | flops | bytes accessed | tf_op | source)
XLA Modules:
  0.0 96.2 jit_solution(7576089705750040686)
XLA Ops:
  0.6 0.0 copy-start
  0.6 1.0 %slice.6 = f32[2,144,256]{2,1,0:T(8,128)S(1)} slice(f32[2,256,256]{2,1,0:T(8,128)} %own_ref.1), slice={[0:2], [0:144], [0:256]} | slice | bytes 589824 | tf_op jit(solution)/shard_map/slice | solution.py:386
  1.7 3.1 %collective-permute-start.1 = (f32[2,144,256]{2,1,0:T(8,128)S(1)}, f32[2,144,256]{2,1,0:T(8,128)S(1)}, u32[]{:S(2)}, u32[]{:S(2)}) collective-permute-start(f32[2,144,256]{2,1,0:T(8,128)S(1)} %slice.6), channel_id=1, source_target_pairs={{8,0},{16,8},{24,16},{9,1},{17,9},{25,17},{10,2},{18,10},{26,18},{... | collective-permute-start | bytes 884744 | tf_op jit(solution)/shard_map/ppermute | solution.py:22
  4.8 0.0 copy-done
  4.8 2.9 %collective-permute-start = (f32[2,256,256]{2,1,0:T(8,128)S(1)}, f32[2,256,256]{2,1,0:T(8,128)S(1)}, u32[]{:S(2)}, u32[]{:S(2)}) collective-permute-start(f32[2,256,256]{2,1,0:T(8,128)S(1)} %copy-done), channel_id=1, source_target_pairs={{1,0},{2,1},{3,2},{4,3},{5,4},{6,5},{7,6},{9,8},{10,9},{11,10},{12... | collective-permute-start | bytes 1572872 | tf_op jit(solution)/shard_map/ppermute | solution.py:22
  7.6 3.8 %collective-permute-done.1.below_first_ref = f32[2,144,256]{2,1,0:T(8,128)S(1)} collective-permute-done((f32[2,144,256]{2,1,0:T(8,128)S(1)}, f32[2,144,256]{2,1,0:T(8,128)S(1)}, u32[]{:S(2)}, u32[]{:S(2)}) %collective-permute-start.1) | collective-permute-done | bytes 294944 | tf_op jit(solution)/shard_map/ppermute | solution.py:22
  11.5 3.4 %collective-permute-start.3 = (f32[2,144,256]{2,1,0:T(8,128)S(1)}, f32[2,144,256]{2,1,0:T(8,128)S(1)}, u32[]{:S(2)}, u32[]{:S(2)}) collective-permute-start(f32[2,144,256]{2,1,0:T(8,128)S(1)} %collective-permute-done.1.below_first_ref), channel_id=1, source_target_pairs={{1,0},{2,1},{3,2},{4,3},{5,4},{6,5},{7,6},{9,8},{10,9},{11,10},{12... | collective-permute-start | bytes 884744 | tf_op jit(solution)/shard_map/ppermute | solution.py:22
  14.9 0.0 copy-start.1
  14.9 4.0 %collective-permute-start.4 = (f32[2,112,256]{2,1,0:T(8,128)S(1)}, f32[2,112,256]{2,1,0:T(8,128)S(1)}, u32[]{:S(2)}, u32[]{:S(2)}) collective-permute-start(f32[2,112,256]{2,1,0:T(8,128)S(1)} %slice.7), channel_id=1, source_target_pairs={{9,0},{10,1},{11,2},{12,3},{13,4},{14,5},{15,6},{17,8},{18,9},{19,... | collective-permute-start | bytes 688136 | tf_op jit(solution)/shard_map/ppermute | solution.py:397
  18.9 2.0 %collective-permute-start.2 = (f32[2,112,256]{2,1,0:T(8,128)S(1)}, f32[2,112,256]{2,1,0:T(8,128)S(1)}, u32[]{:S(2)}, u32[]{:S(2)}) collective-permute-start(f32[2,112,256]{2,1,0:T(8,128)S(1)} %slice.7), channel_id=1, source_target_pairs={{8,0},{16,8},{24,16},{9,1},{17,9},{25,17},{10,2},{18,10},{26,18},{... | collective-permute-start | bytes 688136 | tf_op jit(solution)/shard_map/ppermute | solution.py:22
  21.0 2.7 %prepare.1 = (bf16[768,256]{1,0:T(8,128)(2,1)S(1)}, bf16[256,768]{1,0:T(8,128)(2,1)S(1)}, bf16[256,768]{1,0:T(8,128)(2,1)S(1)}, bf16[768,256]{1,0:T(8,128)(2,1)S...) custom-call(f32[2,256,256]{2,1,0:T(8,128)} %measured_ref.1, ...), custom_call_target="tpu_custom_call" | custom-call | tf_op jit(solution)/shard_map/prepare/pallas_call | solution.py:298
  23.7 1.4 %collective-permute-done.4.corner_last_ref = f32[2,112,256]{2,1,0:T(8,128)S(1)} collective-permute-done((f32[2,112,256]{2,1,0:T(8,128)S(1)}, f32[2,112,256]{2,1,0:T(8,128)S(1)}, u32[]{:S(2)}, u32[]{:S(2)}) %collective-permute-start.4) | collective-permute-done | bytes 229408 | tf_op jit(solution)/shard_map/ppermute | solution.py:397
  25.1 4.2 %collective-permute-done.2.below_last_ref = f32[2,112,256]{2,1,0:T(8,128)S(1)} collective-permute-done((f32[2,112,256]{2,1,0:T(8,128)S(1)}, f32[2,112,256]{2,1,0:T(8,128)S(1)}, u32[]{:S(2)}, u32[]{:S(2)}) %collective-permute-start.2) | collective-permute-done | bytes 229408 | tf_op jit(solution)/shard_map/ppermute | solution.py:22
  29.3 0.0 collective-permute-done.right_ref
  29.3 0.0 collective-permute-done.3.corner_first_ref
  29.3 0.0 copy-done.1
  29.3 9.0 %process_scans.1 = (f32[2,256,256]{2,1,0:T(8,128)S(1)}, f32[2,256,256]{2,1,0:T(8,128)}, f32[2,256,256]{2,1,0:T(8,128)S(1)}, f32[2,256,256]{2,1,0:T(8,128)S(1)}, ...) custom-call(s32[2]{0:T(128)} %down_ref.1, s32[2]{0:T(128)} %across_ref.1, ...), custom_call_target="tpu_custom_call" | custom-call | tf_op jit(solution)/shard_map/process_scans/pallas_call | solution.py:312
  38.3 0.4 collective-permute-start.9
  38.7 1.5 %collective-permute-done.9 = f32[2,256,256]{2,1,0:T(8,128)S(1)} collective-permute-done((f32[2,256,256]{2,1,0:T(8,128)S(1)}, f32[2,256,256]{2,1,0:T(8,128)S(1)}, u32[]{:S(2)}, u32[]{:S(2)}) %collective-permute-start.9) | collective-permute-done | bytes 524320 | tf_op jit(solution)/shard_map/ppermute | solution.py:26
  40.3 0.1 add.6
  40.3 13.1 %all_to_all.10.pieces_ref = f32[8,64,256]{2,1,0:T(8,128)S(1)} all-to-all(f32[8,64,256]{2,1,0:T(8,128)S(1)} %bitcast.4), channel_id=1, replica_groups={{0,2,8,10,16,18,24,26},{1,3,9,11,17,19,25,27},{4,6,12,14,20,22,28,30},{..., dimensions={0} | all-to-all | bytes 1048576 | tf_op jit(solution)/shard_map/all_to_all | solution.py:45
  53.4 1.4 %collective-permute-start.10 = (f32[64,256]{1,0:T(8,128)S(1)}, f32[64,256]{1,0:T(8,128)S(1)}, u32[]{:S(2)}, u32[]{:S(2)}) collective-permute-start(f32[64,256]{1,0:T(8,128)S(1)} %sum_pieces.1), channel_id=1, source_target_pairs={{0,4},{1,5},{2,6},{3,7},{4,0},{5,1},{6,2},{7,3},{8,12},{9,13},{10,... | collective-permute-start | bytes 196616 | tf_op jit(solution)/shard_map/ppermute | solution.py:26
  54.8 2.7 %collective-permute-done.10 = f32[64,256]{1,0:T(8,128)S(1)} collective-permute-done((f32[64,256]{1,0:T(8,128)S(1)}, f32[64,256]{1,0:T(8,128)S(1)}, u32[]{:S(2)}, u32[]{:S(2)}) %collective-permute-start.10) | collective-permute-done | bytes 65568 | tf_op jit(solution)/shard_map/ppermute | solution.py:26
  57.5 0.8 broadcast_in_dim.2
  58.4 4.5 %all-to-all-start.1 = ((f32[8,64,256]{2,1,0:T(8,128)}), f32[8,64,256]{2,1,0:T(8,128)S(1)}, u32[]{:S(2)}, u32[]{:S(2)}) async-start(f32[8,64,256]{2,1,0:T(8,128)} %broadcast_in_dim.2), calls=%async_computation.1 | async-start | bytes 1048576 | tf_op jit(solution)/shard_map/all_to_all | solution.py:50
  62.9 1.3 %collective-permute-start.6 = (f32[2,256,256]{2,1,0:T(8,128)S(1)}, f32[2,256,256]{2,1,0:T(8,128)S(1)}, u32[]{:S(2)}, u32[]{:S(2)}) collective-permute-start(f32[2,256,256]{2,1,0:T(8,128)S(1)} %get-tuple-element.30), channel_id=1, source_target_pairs={{0,1},{2,3},{4,5},{6,7},{8,9},{10,11},{12,13},{14,15},{16,17},{18,... | collective-permute-start | bytes 1572872 | tf_op jit(solution)/shard_map/ppermute | solution.py:422
  64.2 5.3 %collective-permute-start.5 = (f32[2,256,256]{2,1,0:T(8,128)}, f32[2,256,256]{2,1,0:T(8,128)S(1)}, u32[]{:S(2)}, u32[]{:S(2)}) collective-permute-start(f32[2,256,256]{2,1,0:T(8,128)} %get-tuple-element.28), channel_id=1, source_target_pairs={{0,1},{1,2},{2,3},{3,4},{4,5},{5,6},{6,7},{8,9},{9,10},{10,11},{11... | collective-permute-start | bytes 1572872 | tf_op jit(solution)/shard_map/ppermute | solution.py:22
  69.5 2.9 %collective-permute-start.8 = (f32[2,256,256]{2,1,0:T(8,128)}, f32[2,256,256]{2,1,0:T(8,128)S(1)}, u32[]{:S(2)}, u32[]{:S(2)}) collective-permute-start(f32[2,256,256]{2,1,0:T(8,128)} %get-tuple-element.31), channel_id=1, source_target_pairs={{1,10},{3,12},{5,14},{9,18},{11,20},{13,22},{17,26},{19,28},{21,30}} | collective-permute-start | bytes 1572872 | tf_op jit(solution)/shard_map/ppermute | solution.py:426
  72.3 0.0 collective-permute-done.6.refs_1_
  72.3 0.1 add_tiles.2
  72.4 1.9 %collective-permute-start.7 = (f32[2,256,256]{2,1,0:T(8,128)S(1)}, f32[2,256,256]{2,1,0:T(8,128)S(1)}, u32[]{:S(2)}, u32[]{:S(2)}) collective-permute-start(f32[2,256,256]{2,1,0:T(8,128)S(1)} %add_tiles.2), channel_id=1, source_target_pairs={{0,8},{8,16},{16,24},{1,9},{9,17},{17,25},{2,10},{10,18},{18,26},{... | collective-permute-start | bytes 1572872 | tf_op jit(solution)/shard_map/ppermute | solution.py:22
  74.3 0.0 all-to-all-done.1
  74.3 0.3 collective-permute-start.11
  74.7 1.2 %collective-permute-done.5.refs_1_ = f32[2,256,256]{2,1,0:T(8,128)S(1)} collective-permute-done((f32[2,256,256]{2,1,0:T(8,128)}, f32[2,256,256]{2,1,0:T(8,128)S(1)}, u32[]{:S(2)}, u32[]{:S(2)}) %collective-permute-start.5) | collective-permute-done | bytes 524320 | tf_op jit(solution)/shard_map/ppermute | solution.py:22
  75.9 5.7 %collective-permute-done.8.refs_3_ = f32[2,256,256]{2,1,0:T(8,128)S(1)} collective-permute-done((f32[2,256,256]{2,1,0:T(8,128)}, f32[2,256,256]{2,1,0:T(8,128)S(1)}, u32[]{:S(2)}, u32[]{:S(2)}) %collective-permute-start.8) | collective-permute-done | bytes 524320 | tf_op jit(solution)/shard_map/ppermute | solution.py:426
  81.6 12.2 %collective-permute-done.7.refs_2_ = f32[2,256,256]{2,1,0:T(8,128)S(1)} collective-permute-done((f32[2,256,256]{2,1,0:T(8,128)S(1)}, f32[2,256,256]{2,1,0:T(8,128)S(1)}, u32[]{:S(2)}, u32[]{:S(2)}) %collective-permute-start.7) | collective-permute-done | bytes 524320 | tf_op jit(solution)/shard_map/ppermute | solution.py:22
  93.7 0.9 add_tiles.3
  94.6 0.8 place_mode.2.refs_0_
  95.4 0.0 collective-permute-done.11.values_ref
  95.4 0.8 place_mode.3
  (3 shorter events, 0.1 us)
Async XLA Ops:
  0.6 4.1 %copy-start = (f32[2,256,256]{2,1,0:T(8,128)S(1)}, f32[2,256,256]{2,1,0:T(8,128)}, u32[]{:S(2)}) copy-start(f32[2,256,256]{2,1,0:T(8,128)} %own_ref.1) | copy-start | bytes 1572868
  1.7 9.8 %collective-permute-start.1 = (f32[2,144,256]{2,1,0:T(8,128)S(1)}, f32[2,144,256]{2,1,0:T(8,128)S(1)}, u32[]{:S(2)}, u32[]{:S(2)}) collective-permute-start(f32[2,144,256]{2,1,0:T(8,128)S(1)} %slice.6), channel_id=1, source_target_pairs={{8,0},{16,8},{24,16},{9,1},{17,9},{25,17},{10,2},{18,10},{26,18},{... | collective-permute-start | bytes 884744 | tf_op jit(solution)/shard_map/ppermute | solution.py:22
  4.8 24.5 %collective-permute-start = (f32[2,256,256]{2,1,0:T(8,128)S(1)}, f32[2,256,256]{2,1,0:T(8,128)S(1)}, u32[]{:S(2)}, u32[]{:S(2)}) collective-permute-start(f32[2,256,256]{2,1,0:T(8,128)S(1)} %copy-done), channel_id=1, source_target_pairs={{1,0},{2,1},{3,2},{4,3},{5,4},{6,5},{7,6},{9,8},{10,9},{11,10},{12... | collective-permute-start | bytes 1572872 | tf_op jit(solution)/shard_map/ppermute | solution.py:22
  11.5 17.8 %collective-permute-start.3 = (f32[2,144,256]{2,1,0:T(8,128)S(1)}, f32[2,144,256]{2,1,0:T(8,128)S(1)}, u32[]{:S(2)}, u32[]{:S(2)}) collective-permute-start(f32[2,144,256]{2,1,0:T(8,128)S(1)} %collective-permute-done.1.below_first_ref), channel_id=1, source_target_pairs={{1,0},{2,1},{3,2},{4,3},{5,4},{6,5},{7,6},{9,8},{10,9},{11,10},{12... | collective-permute-start | bytes 884744 | tf_op jit(solution)/shard_map/ppermute | solution.py:22
  14.9 14.4 %copy-start.1 = (f32[2,2,256,256]{3,2,1,0:T(8,128)S(1)}, f32[2,2,256,256]{3,2,1,0:T(8,128)}, u32[]{:S(2)}) copy-start(f32[2,2,256,256]{3,2,1,0:T(8,128)} %probe_ref.1) | copy-start | bytes 3145732
  14.9 10.2 %collective-permute-start.4 = (f32[2,112,256]{2,1,0:T(8,128)S(1)}, f32[2,112,256]{2,1,0:T(8,128)S(1)}, u32[]{:S(2)}, u32[]{:S(2)}) collective-permute-start(f32[2,112,256]{2,1,0:T(8,128)S(1)} %slice.7), channel_id=1, source_target_pairs={{9,0},{10,1},{11,2},{12,3},{13,4},{14,5},{15,6},{17,8},{18,9},{19,... | collective-permute-start | bytes 688136 | tf_op jit(solution)/shard_map/ppermute | solution.py:397
  18.9 10.4 %collective-permute-start.2 = (f32[2,112,256]{2,1,0:T(8,128)S(1)}, f32[2,112,256]{2,1,0:T(8,128)S(1)}, u32[]{:S(2)}, u32[]{:S(2)}) collective-permute-start(f32[2,112,256]{2,1,0:T(8,128)S(1)} %slice.7), channel_id=1, source_target_pairs={{8,0},{16,8},{24,16},{9,1},{17,9},{25,17},{10,2},{18,10},{26,18},{... | collective-permute-start | bytes 688136 | tf_op jit(solution)/shard_map/ppermute | solution.py:22
  38.3 1.9 %collective-permute-start.9 = (f32[2,256,256]{2,1,0:T(8,128)S(1)}, f32[2,256,256]{2,1,0:T(8,128)S(1)}, u32[]{:S(2)}, u32[]{:S(2)}) collective-permute-start(f32[2,256,256]{2,1,0:T(8,128)S(1)} %get-tuple-element.33), channel_id=1, source_target_pairs={{0,1},{1,0},{2,3},{3,2},{4,5},{5,4},{6,7},{7,6},{8,9},{9,8},{10,11... | collective-permute-start | bytes 1572872 | tf_op jit(solution)/shard_map/ppermute | solution.py:26
  53.4 4.1 %collective-permute-start.10 = (f32[64,256]{1,0:T(8,128)S(1)}, f32[64,256]{1,0:T(8,128)S(1)}, u32[]{:S(2)}, u32[]{:S(2)}) collective-permute-start(f32[64,256]{1,0:T(8,128)S(1)} %sum_pieces.1), channel_id=1, source_target_pairs={{0,4},{1,5},{2,6},{3,7},{4,0},{5,1},{6,2},{7,3},{8,12},{9,13},{10,... | collective-permute-start | bytes 196616 | tf_op jit(solution)/shard_map/ppermute | solution.py:26
  58.4 16.0 %all-to-all-start.1 = ((f32[8,64,256]{2,1,0:T(8,128)}), f32[8,64,256]{2,1,0:T(8,128)S(1)}, u32[]{:S(2)}, u32[]{:S(2)}) async-start(f32[8,64,256]{2,1,0:T(8,128)} %broadcast_in_dim.2), calls=%async_computation.1 | async-start | bytes 1048576 | tf_op jit(solution)/shard_map/all_to_all | solution.py:50
  62.9 9.5 %collective-permute-start.6 = (f32[2,256,256]{2,1,0:T(8,128)S(1)}, f32[2,256,256]{2,1,0:T(8,128)S(1)}, u32[]{:S(2)}, u32[]{:S(2)}) collective-permute-start(f32[2,256,256]{2,1,0:T(8,128)S(1)} %get-tuple-element.30), channel_id=1, source_target_pairs={{0,1},{2,3},{4,5},{6,7},{8,9},{10,11},{12,13},{14,15},{16,17},{18,... | collective-permute-start | bytes 1572872 | tf_op jit(solution)/shard_map/ppermute | solution.py:422
  64.2 11.7 %collective-permute-start.5 = (f32[2,256,256]{2,1,0:T(8,128)}, f32[2,256,256]{2,1,0:T(8,128)S(1)}, u32[]{:S(2)}, u32[]{:S(2)}) collective-permute-start(f32[2,256,256]{2,1,0:T(8,128)} %get-tuple-element.28), channel_id=1, source_target_pairs={{0,1},{1,2},{2,3},{3,4},{4,5},{5,6},{6,7},{8,9},{9,10},{10,11},{11... | collective-permute-start | bytes 1572872 | tf_op jit(solution)/shard_map/ppermute | solution.py:22
  69.5 12.1 %collective-permute-start.8 = (f32[2,256,256]{2,1,0:T(8,128)}, f32[2,256,256]{2,1,0:T(8,128)S(1)}, u32[]{:S(2)}, u32[]{:S(2)}) collective-permute-start(f32[2,256,256]{2,1,0:T(8,128)} %get-tuple-element.31), channel_id=1, source_target_pairs={{1,10},{3,12},{5,14},{9,18},{11,20},{13,22},{17,26},{19,28},{21,30}} | collective-permute-start | bytes 1572872 | tf_op jit(solution)/shard_map/ppermute | solution.py:426
  72.4 21.3 %collective-permute-start.7 = (f32[2,256,256]{2,1,0:T(8,128)S(1)}, f32[2,256,256]{2,1,0:T(8,128)S(1)}, u32[]{:S(2)}, u32[]{:S(2)}) collective-permute-start(f32[2,256,256]{2,1,0:T(8,128)S(1)} %add_tiles.2), channel_id=1, source_target_pairs={{0,8},{8,16},{16,24},{1,9},{9,17},{17,25},{2,10},{10,18},{18,26},{... | collective-permute-start | bytes 1572872 | tf_op jit(solution)/shard_map/ppermute | solution.py:22
  74.3 21.1 %collective-permute-start.11 = (f32[2,256,256]{2,1,0:T(8,128)S(1)}, f32[2,256,256]{2,1,0:T(8,128)S(1)}, u32[]{:S(2)}, u32[]{:S(2)}) collective-permute-start(f32[2,256,256]{2,1,0:T(8,128)S(1)} %bitcast.2), channel_id=1, source_target_pairs={{0,1},{1,0},{2,3},{3,2},{4,5},{5,4},{6,7},{7,6},{8,9},{9,8},{10,11... | collective-permute-start | bytes 1572872 | tf_op jit(solution)/shard_map/ppermute | solution.py:26
